TPU v7x, 256 devices: a whole 4x4x8 slice. The times are simulated.
256 devices in a mesh: clus: 16 (over x, y), leaf: 16 (over z, core).
Axes of the slice: x: 4, y: 4, z: 8, core: 2. Of those that a mesh axis runs over, the one named last changes fastest.
Arguments:
- points: bfloat16 [64, 524288], P(None, ('clus', 'leaf')), may hold values from -6 to 6
- weights: bfloat16 [512, 524288], P(None, ('clus', 'leaf')), may hold values from -2 to 2
- targets: bfloat16 [512, 524288], P(None, ('clus', 'leaf')), may hold values from -6 to 6
- near_lists: int32 [1024, 4], P(('clus', 'leaf')), may hold values from 0 to 1023, as said below
- tile_counts: int32 [1024], P(('clus', 'leaf')), may hold values from 2 to 4, as said below
- skeleton: int32 [256, 256], P(('clus', 'leaf')), may hold values from 0 to 2047, as said below
Outputs:
- precond: float32 [512, 524288], P(None, ('clus', 'leaf'))
Inputs may be any that keep to these rules, and one draw needn't show every extreme that they name: `near_lists`: row g lists cluster ids; its first entry is g; its first tile_counts[g] entries are distinct, and the rest repeat g. Every listed cluster lies on a device with the same leaf index as cluster g's device and a clus index at most 1 away; some cluster lists one exactly 1 away. `tile_counts`: some cluster has exactly 4 tiles. `skeleton`: each row holds 256 distinct indices of points of its device; their order matters.
All inputs are finite; a program needn't handle non-finite values.
Results may differ from a plain program's by a relative error of at most 0.0039.
Values may be sent and summed in bfloat16 or wider, within the bound.
No kernel may reach another device: no remote copies, remote signals or barrier semaphores. Data moves between devices by JAX's collectives and lax.ppermute only.
A program may use at most 128 MiB of HBM per device.

v0:
```python
import functools

import jax
import jax.numpy as jnp
from jax import lax
from jax.experimental import pallas as pl
from jax.experimental.pallas import tpu as pltpu
from jax.sharding import PartitionSpec as P


CLUSTER_PTS = 512
N_LEAF = 16
RIDGE = 0.5
SHIFT = 4.0
EARLY_ROWS = 192
COARSE_STEPS = 4
FINE_STEPS = 2

f32 = jnp.float32
bf16 = jnp.bfloat16
MIB = 1 << 20
VMEM = pl.BlockSpec(memory_space=pltpu.VMEM)
SMEM = pl.BlockSpec(memory_space=pltpu.SMEM)


def mm(a, b):
    return jnp.dot(a, b, preferred_element_type=f32)


def split(a):
    high = a.astype(bf16)
    return high, (a - high.astype(f32)).astype(bf16)


def lifted(x):
    wide = x.astype(f32)
    half = -0.5 * jnp.sum(wide * wide, axis=0, keepdims=True)
    high = half.astype(bf16).astype(f32)
    rest = half - high
    mid = rest.astype(bf16).astype(f32)
    low = rest - mid
    row = lax.broadcasted_iota(jnp.int32, (16, x.shape[1]), 0)

    def tail(at, ones):
        out = jnp.where((row >= ones) & (row < ones + 3), 1.0, 0.0)
        out = jnp.where(row == at, high, out)
        out = jnp.where(row == at + 1, mid, out)
        return jnp.where(row == at + 2, low, out).astype(bf16)

    left = jnp.concatenate([x, tail(0, 3)], axis=0)
    right = jnp.concatenate([x, tail(3, 0)], axis=0)
    return left, right


def kernel_of(left, right, features):
    half = lax.dot_general(left, right, (((0,), (0,)), ((), ())), preferred_element_type=f32)
    return jnp.exp((4.0 / features) * half)


def leaf_of(lists):
    return (lists[0, 0] // lists.shape[0]) % N_LEAF


def params(mib=24):
    return pltpu.CompilerParams(vmem_limit_bytes=mib * MIB)


def prep_kernel(*refs):
    srcs, (pick, note, kept), dsts, sems = refs[:4], refs[4:7], refs[7:11], refs[11]
    copies = [pltpu.make_async_copy(a, b, sems.at[k]) for k, (a, b) in enumerate(zip(srcs, dsts))]
    for copy in copies:
        copy.start()
    for copy in copies:
        copy.wait()
    lists, counts, pts, skel = dsts
    features, n = pts.shape
    s = skel.shape[1]
    clusters, slots = lists.shape
    chosen = skel[...]
    row = lax.broadcasted_iota(jnp.int32, (n, s), 0)
    picked = jnp.where(row == chosen, 1.0, 0.0).astype(bf16)
    pick[...] = picked
    gathered = mm(pts[...], picked).astype(bf16)
    note[:features, :] = gathered
    kept[...] = gathered[:, : s // 2]
    home = chosen // CLUSTER_PTS
    line = lax.broadcasted_iota(jnp.int32, (16, s), 0)
    flags = jnp.zeros((16, s), f32)
    for g in range(clusters):
        for slot in range(slots):
            listed = lists[g, slot]
            way = listed // clusters - lists[0, 0] // clusters
            begin = jnp.where(way < 0, 0, jnp.where(way > 0, clusters, 2 * clusters))
            at = jnp.where(slot < counts[g], begin + listed % clusters, -1)
            flags = jnp.where((line == at) & (home == g), 1.0, flags)
    note[features:, :] = flags.astype(bf16)


def prep(near_lists, tile_counts, points, skeleton):
    features, n = points.shape
    s = skeleton.shape[1]
    return pl.pallas_call(
        prep_kernel,
        out_shape=(
            jax.ShapeDtypeStruct((n, s), bf16),
            jax.ShapeDtypeStruct((features + 16, s), bf16),
            jax.ShapeDtypeStruct((features, s // 2), bf16),
        ),
        in_specs=[pl.BlockSpec(memory_space=pltpu.HBM)] * 4,
        out_specs=(VMEM, VMEM, VMEM),
        scratch_shapes=[
            pltpu.SMEM(near_lists.shape, jnp.int32),
            pltpu.SMEM(tile_counts.shape, jnp.int32),
            pltpu.VMEM(points.shape, bf16),
            pltpu.VMEM(skeleton.shape, jnp.int32),
            pltpu.SemaphoreType.DMA((4,)),
        ],
        compiler_params=params(),
        name="prep",
    )(near_lists, tile_counts, points, skeleton)


def invert(grams, between=()):
    between = list(between)
    share = -(-len(between) // (COARSE_STEPS + FINE_STEPS))

    def work():
        for _ in range(share):
            if between:
                between.pop(0)()

    s = grams[0].shape[0]
    eye = jnp.where(
        lax.broadcasted_iota(jnp.int32, (s, s), 0) == lax.broadcasted_iota(jnp.int32, (s, s), 1),
        1.0,
        0.0,
    ).astype(f32)
    parts, guesses, gaps = [], [], []
    for gram in grams:
        gram = gram + SHIFT * eye
        top = jnp.max(jnp.sum(gram, axis=0, keepdims=True), axis=1, keepdims=True)
        alpha = 2.0 / (top + SHIFT)
        gap = (top - SHIFT) / (top + SHIFT)
        gain = 2.0 / (2.0 - gap * gap)
        parts.append(split(gram))
        guesses.append((gain * alpha) * (2.0 * eye - alpha * gram))
        gaps.append(0.5 * gain * gap * gap)
    for _ in range(COARSE_STEPS):
        lows = [x.astype(bf16) for x in guesses]
        prods = [mm(gh, x) + mm(gl, x) for (gh, gl), x in zip(parts, lows)]
        work()
        gains = [2.0 / (2.0 - gap * gap) for gap in gaps]
        guesses = [
            gain * mm(x, (2.0 * eye - p).astype(bf16)) for gain, x, p in zip(gains, lows, prods)
        ]
        gaps = [0.5 * gain * gap * gap for gain, gap in zip(gains, gaps)]
    for _ in range(FINE_STEPS):
        splits = [split(x) for x in guesses]
        prods = [
            mm(gh, xh) + (mm(gh, xl) + mm(gl, xh)) for (gh, gl), (xh, xl) in zip(parts, splits)
        ]
        work()
        guesses = [
            x + mm(xh, (eye - p).astype(bf16)) for x, (xh, _), p in zip(guesses, splits, prods)
        ]
    while between:
        between.pop(0)()
    return guesses


def tree_part(total, w, left, right, ref, begin, j):
    features = ref.shape[0] - 16
    cols = slice(j * CLUSTER_PTS, (j + 1) * CLUSTER_PTS)
    flags = ref[features + begin + j : features + begin + j + 1, :].astype(f32)
    tile = kernel_of(left[:, cols], right, features) * flags
    term = mm(w[:, cols], tile.astype(bf16))
    if j == 0:
        total[...] = term
    else:
        total[...] += term


def solve_rows(values, high, low):
    vh, vl = split(values)
    return mm(vh, high) + (mm(vh, low) + mm(vl, high))


def inverse_kernel(pts, w, targets, pick, note, kept, o1, o2, o3, o4, mine, a_high, a_low, b_high, b_low, left, total):
    features, half = kept.shape
    clusters = pts.shape[1] // CLUSTER_PTS
    left[...] = lifted(pts[...])[0]
    own = kept[...]
    node_left, node_right = lifted(note[:features, :])
    grams = [kernel_of(node_left, node_right, features)]
    for other in (o1, o2, o3, o4):
        pair_left, pair_right = lifted(jnp.concatenate([own, other[...]], axis=1))
        grams.append(kernel_of(pair_left, pair_right, features))
    jobs = [
        functools.partial(tree_part, total, w, left, node_right, note, 2 * clusters, j)
        for j in range(clusters)
    ]

    def rest():
        total[...] = mm(targets[...], pick[...]) - RIDGE * mm(w[...], pick[...]) - total[...]

    found = invert(grams, jobs + [rest])
    ah, al = split(found[0])
    a_high[...], a_low[...] = ah, al
    for k in range(4):
        b_high[k], b_low[k] = split(SHIFT * found[k + 1][:, :half])
    mine[...] = solve_rows(total[...], ah[:, :half], al[:, :half])


def inverses(points, weights, targets, pick, note, kept, others):
    features, n = points.shape
    rows = weights.shape[0]
    half = kept.shape[1]
    s = 2 * half
    part = jax.ShapeDtypeStruct((4, s, half), bf16)
    full = jax.ShapeDtypeStruct((s, s), bf16)
    return pl.pallas_call(
        inverse_kernel,
        out_shape=(jax.ShapeDtypeStruct((rows, half), f32), full, full, part, part),
        in_specs=[VMEM] * 10,
        out_specs=(VMEM,) * 5,
        scratch_shapes=[pltpu.VMEM((features + 16, n), bf16), pltpu.VMEM((rows, s), f32)],
        compiler_params=params(),
        name="inverses",
    )(points, weights, targets, pick, note, kept, *others)


def push_kernel(pts, w, note_b, note_a, to_b, to_a, left, total):
    features, n = pts.shape
    half = to_b.shape[1]
    clusters = n // CLUSTER_PTS
    left[...] = lifted(pts[...])[0]
    notes = ((note_b, clusters), (note_a, 0))
    grams, jobs = [], []
    for k, (ref, begin) in enumerate(notes):
        node_left, node_right = lifted(ref[:features, :])
        grams.append(kernel_of(node_left, node_right, features))
        jobs += [
            functools.partial(tree_part, total.at[k], w, left, node_right, ref, begin, j)
            for j in range(clusters)
        ]
    for k, found in enumerate(invert(grams, jobs)):
        high, low = split(found[:, :half])
        (to_b, to_a)[k][...] = solve_rows(total[k], high, low)


def push(points, weights, note_b, note_a):
    features, n = points.shape
    rows = weights.shape[0]
    s = note_b.shape[1]
    return pl.pallas_call(
        push_kernel,
        out_shape=(jax.ShapeDtypeStruct((rows, s // 2), f32),) * 2,
        in_specs=[VMEM] * 4,
        out_specs=(VMEM,) * 2,
        scratch_shapes=[pltpu.VMEM((features + 16, n), bf16), pltpu.VMEM((2, rows, s), f32)],
        compiler_params=params(),
        name="push",
    )(points, weights, note_b, note_a)


def join_kernel(mine, from_b, from_a, out):
    out[...] = mine[...] - from_b[...] - from_a[...]


def join(mine, from_b, from_a):
    return pl.pallas_call(
        join_kernel,
        out_shape=jax.ShapeDtypeStruct(mine.shape, f32),
        in_specs=[VMEM] * 3,
        out_specs=VMEM,
        compiler_params=params(),
        name="join",
    )(mine, from_b, from_a)


def pair_of(lists, counts, i):
    slots = lists.shape[1]
    clusters = lists.shape[0]
    g = i // slots
    listed = lists[g, i % slots]
    way = listed // clusters - lists[0, 0] // clusters
    cols = pl.multiple_of((listed % clusters) * CLUSTER_PTS, CLUSTER_PTS)
    own_cols = pl.multiple_of(g * CLUSTER_PTS, CLUSTER_PTS)
    return (i % slots) < counts[g], way, pl.ds(cols, CLUSTER_PTS), pl.ds(own_cols, CLUSTER_PTS)


def own_kernel(lists, counts, pts, note, w, targets, pick, out, spread_tile, place, left, right, tile):
    features = pts.shape[0]
    left[...], right[...] = lifted(pts[...])
    node_left = lifted(note[:features, :])[0]
    spread_tile[...] = kernel_of(node_left, right[...], features).astype(bf16)
    place[...] = pick[...].T
    out[...] = targets[...].astype(f32) - RIDGE * w[...].astype(f32)

    def step(i, carry):
        live, way, cols, own = pair_of(lists, counts, i)

        @pl.when(live & (way == 0))
        def _():
            tile[...] = kernel_of(left[:, cols], right[:, own], features).astype(bf16)
            out[:, own] -= mm(w[:, cols], tile[...])

        return carry

    lax.fori_loop(0, lists.shape[0] * lists.shape[1], step, 0)


def own_near(points, note, weights, targets, pick, near_lists, tile_counts):
    features, n = points.shape
    return pl.pallas_call(
        own_kernel,
        out_shape=(
            jax.ShapeDtypeStruct(weights.shape, f32),
            jax.ShapeDtypeStruct((note.shape[1], n), bf16),
            jax.ShapeDtypeStruct((note.shape[1], n), bf16),
        ),
        in_specs=[SMEM, SMEM] + [VMEM] * 5,
        out_specs=(VMEM, VMEM, VMEM),
        scratch_shapes=[
            pltpu.VMEM((features + 16, n), bf16),
            pltpu.VMEM((features + 16, n), bf16),
            pltpu.VMEM((CLUSTER_PTS, CLUSTER_PTS), bf16),
        ],
        compiler_params=params(),
        name="own_near",
    )(near_lists, tile_counts, points, note, weights, targets, pick)


def tiles_kernel(lists, counts, pts, before, after, out, lb, la, right):
    features = pts.shape[0]
    right[...] = lifted(pts[...])[1]
    lb[...] = lifted(before[...])[0]
    la[...] = lifted(after[...])[0]

    def step(i, carry):
        live, way, cols, own = pair_of(lists, counts, i)

        @pl.when(live & (way < 0))
        def _():
            out[i] = kernel_of(lb[:, cols], right[:, own], features).astype(bf16)

        @pl.when(live & (way > 0))
        def _():
            out[i] = kernel_of(la[:, cols], right[:, own], features).astype(bf16)

        return carry

    lax.fori_loop(0, lists.shape[0] * lists.shape[1], step, 0)


def near_tiles(points, before, after, near_lists, tile_counts):
    features, n = points.shape
    pairs = near_lists.shape[0] * near_lists.shape[1]
    head = pl.BlockSpec((features, n), lambda i: (0, 0))
    return pl.pallas_call(
        tiles_kernel,
        out_shape=jax.ShapeDtypeStruct((pairs, CLUSTER_PTS, CLUSTER_PTS), bf16),
        grid=(1,),
        in_specs=[SMEM, SMEM, VMEM, head, head],
        out_specs=VMEM,
        scratch_shapes=[pltpu.VMEM((features + 16, n), bf16)] * 3,
        compiler_params=params(),
        name="near_tiles",
    )(near_lists, tile_counts, points, before, after)


def near_kernel(first, skip, lists, counts, base, before, after, tiles, pick, a_high, a_low, res, sol):
    rows = res.shape[0]
    res[...] = base[first : first + rows, :]

    def step(i, carry):
        live, way, cols, own = pair_of(lists, counts, i)

        @pl.when(live & (way < 0))
        def _():
            res[:, own] -= mm(before[skip : skip + rows, cols], tiles[i])

        @pl.when(live & (way > 0))
        def _():
            res[:, own] -= mm(after[skip : skip + rows, cols], tiles[i])

        return carry

    lax.fori_loop(0, lists.shape[0] * lists.shape[1], step, 0)
    high, low = split(res[...])
    node = mm(jnp.concatenate([high, low], axis=0), pick[...]).astype(bf16)
    both = mm(node, a_high[...])
    sol[...] = both[:rows] + (mm(node[:rows], a_low[...]) + both[rows:])


def near_part(first, rows, skip, base, before, after, tiles, pick, a_high, a_low, near_lists, tile_counts):
    n = base.shape[1]
    s = pick.shape[1]
    return pl.pallas_call(
        functools.partial(near_kernel, first, skip),
        out_shape=(jax.ShapeDtypeStruct((rows, n), f32), jax.ShapeDtypeStruct((rows, s), f32)),
        in_specs=[SMEM, SMEM] + [VMEM] * 7,
        out_specs=(VMEM, VMEM),
        compiler_params=params(),
        name="near_part",
    )(near_lists, tile_counts, base, before, after, tiles, pick, a_high, a_low)


def joint(own, other, b_high, b_low, at):
    half = own.shape[1]
    total = None
    for begin, piece in ((0, own), (half, other)):
        high, low = split(piece[...])
        bh = b_high[at, begin : begin + half, :]
        bl = b_low[at, begin : begin + half, :]
        term = mm(high, bh) + (mm(high, bl) + mm(low, bh))
        total = term if total is None else total + term
    return total


def level_kernel(at, own, other, b_high, b_low, out):
    out[...] = joint(own, other, b_high, b_low, at)


def level_step(at, own, other, b_high, b_low):
    return pl.pallas_call(
        functools.partial(level_kernel, at),
        out_shape=jax.ShapeDtypeStruct(own.shape, f32),
        in_specs=[VMEM] * 4,
        out_specs=VMEM,
        compiler_params=params(),
        name="level_step",
    )(own, other, b_high, b_low)


def among_leaves(value, pairs):
    return lax.ppermute(value, "leaf", pairs)


def out_kernel(cuts, lists, *refs):
    parts = refs[: 2 * len(cuts)]
    v1, v2, v3, w4, b_high, b_low, tile, place, out, buf, sems = refs[2 * len(cuts) :]
    half = v1.shape[1]
    leaf = leaf_of(lists)
    inject = v1[...]
    inject = inject + jnp.where(leaf % 2 == 0, v2[...], 0.0)
    inject = inject + jnp.where(leaf % 4 == 0, v3[...], 0.0)
    inject = inject + jnp.where(leaf % 8 == 0, joint(v3, w4, b_high, b_low, 3), 0.0)
    copies = []
    at = 0
    for k, blocks in enumerate(cuts):
        res, sol = parts[2 * k : 2 * k + 2]
        inner = 0
        for rows in blocks:
            solved = sol[inner : inner + rows, :]
            corr = jnp.concatenate([solved[:, :half] + inject[at : at + rows], solved[:, half:]], axis=1)
            high, low = split(corr)
            spread = mm(high, tile[...])
            spread = spread + mm(high, place[...]) + mm(low, place[...])
            buf[at : at + rows, :] = res[inner : inner + rows, :] * (1.0 / (1.0 + RIDGE)) + spread
            copy = pltpu.make_async_copy(
                buf.at[pl.ds(at, rows)], out.at[pl.ds(at, rows)], sems.at[len(copies)]
            )
            copy.start()
            copies.append(copy)
            at += rows
            inner += rows
    for copy in copies:
        copy.wait()


def finish(cuts, near_lists, parts, rest):
    total = sum(sum(blocks) for blocks in cuts)
    count = sum(len(blocks) for blocks in cuts)
    n = parts[0].shape[1]
    return pl.pallas_call(
        functools.partial(out_kernel, cuts),
        out_shape=jax.ShapeDtypeStruct((total, n), f32),
        in_specs=[SMEM] + [VMEM] * (len(parts) + len(rest)),
        out_specs=pl.BlockSpec(memory_space=pl.ANY),
        scratch_shapes=[pltpu.VMEM((total, n), f32), pltpu.SemaphoreType.DMA((count,))],
        compiler_params=params(),
        name="finish",
    )(near_lists, *parts, *rest)


def shifted(value, by):
    size = lax.axis_size("clus")
    pairs = [(i, i + by) for i in range(size) if 0 <= i + by < size]
    return lax.ppermute(value, "clus", pairs)


def both_ways(value):
    return shifted(value, 1), shifted(value, -1)


def on_device(points, weights, targets, near_lists, tile_counts, skeleton):
    features = points.shape[0]
    rows = weights.shape[0]
    late = rows - EARLY_ROWS
    size = lax.axis_size("leaf")
    steps = [[(i, i ^ (1 << k)) for i in range(0, size, 1 << k)] for k in range(4)]

    pick, note, kept = prep(near_lists, tile_counts, points, skeleton)
    note_b, note_a = both_ways(note)
    first = jnp.concatenate([points, weights[:EARLY_ROWS]], axis=0)
    before_1, after_1 = both_ways(first)
    to_b, to_a = push(points, weights, note_b, note_a)
    from_b = shifted(to_a, 1)
    from_a = shifted(to_b, -1)
    second = weights[EARLY_ROWS:]
    before_2, after_2 = both_ways(second)
    swaps = [[(i, i ^ (1 << k)) for i in range(size)] for k in range(4)]
    others = [among_leaves(kept, swaps[k]) for k in range(4)]
    mine, a_high, a_low, b_high, b_low = inverses(
        points, weights, targets, pick, note, kept, others
    )
    v0 = join(mine, from_b, from_a)

    base, tile, place = own_near(points, note, weights, targets, pick, near_lists, tile_counts)
    tiles = near_tiles(points, before_1, after_1, near_lists, tile_counts)
    shared = (tiles, pick, a_high, a_low, near_lists, tile_counts)
    res_1, sol_1 = near_part(0, EARLY_ROWS, features, base, before_1, after_1, *shared)
    res_2, sol_2 = near_part(EARLY_ROWS, late, 0, base, before_2, after_2, *shared)

    v1 = level_step(0, v0, among_leaves(v0, steps[0]), b_high, b_low)
    v2 = level_step(1, v1, among_leaves(v1, steps[1]), b_high, b_low)
    v3 = level_step(2, v2, among_leaves(v2, steps[2]), b_high, b_low)
    w4 = among_leaves(v3, steps[3])
    cuts = ((EARLY_ROWS,), (late // 2, late // 2))
    return finish(
        cuts, near_lists, (res_1, sol_1, res_2, sol_2), (v1, v2, v3, w4, b_high, b_low, tile, place)
    )


def solution(mesh):
    split_cols = P(None, ("clus", "leaf"))
    split_rows = P(("clus", "leaf"), None)
    placed = (split_cols, split_cols, split_cols, split_rows, P(("clus", "leaf")), split_rows)

    return jax.shard_map(
        on_device, mesh=mesh, in_specs=placed, out_specs=split_cols, check_vma=False
    )
```

profile of v0, /device:TPU:6, one launch (start us, length us, event | category | flops | bytes accessed | tf_op | source)
XLA Modules:
  0.0 110.7 jit_solution(6353310935707236695)
XLA Ops:
  0.0 0.9 copy-done.2
  1.0 0.7 copy-done.6
  1.6 0.7 copy-done.8
  2.3 0.7 copy-done.10
  3.0 1.2 %prep.1 = (bf16[2048,256]{1,0:T(8,128)(2,1)S(1)}, bf16[80,256]{1,0:T(8,128)(2,1)S(1)}, bf16[64,128]{1,0:T(8,128)(2,1)S(1)}) custom-call(s32[4,4]{1,0:T(4,128)S(1)} %copy-done.6, s32[4]{0:T(128)S(1)} %copy-done.8, bf16[64,2048]{1,0:T(8,128)(2,1)S(1)} %copy-done.2, s32[1,256]{1,0:T(1,128)S(1)} %copy-done.10), custom_call_target="tpu_custom_call" | custom-call | tf_op jit(solution)/shard_map/prep/pallas_call | solution.py:102
  4.1 3.5 %collective-permute-start.8 = (bf16[80,256]{1,0:T(8,128)(2,1)S(1)}, bf16[80,256]{1,0:T(8,128)(2,1)S(1)}, u32[]{:S(2)}, u32[]{:S(2)}) collective-permute-start(bf16[80,256]{1,0:T(8,128)(2,1)S(1)} %get-tuple-element.22.note), channel_id=1, source_target_pairs={{0,16},{16,32},{32,48},{48,64},{64,80},{80,96},{96,112},{112,128},... | collective-permute-start | bytes 122888 | tf_op jit(solution)/shard_map/ppermute | solution.py:490
  7.6 4.5 %collective-permute-start.9 = (bf16[80,256]{1,0:T(8,128)(2,1)S(1)}, bf16[80,256]{1,0:T(8,128)(2,1)S(1)}, u32[]{:S(2)}, u32[]{:S(2)}) collective-permute-start(bf16[80,256]{1,0:T(8,128)(2,1)S(1)} %get-tuple-element.22.note), channel_id=1, source_target_pairs={{16,0},{32,16},{48,32},{64,48},{80,64},{96,80},{112,96},{128,112},... | collective-permute-start | bytes 122888 | tf_op jit(solution)/shard_map/ppermute | solution.py:490
  12.1 0.1 collective-permute-start.2
  12.2 2.0 %collective-permute-start.3 = (bf16[64,128]{1,0:T(8,128)(2,1)S(1)}, bf16[64,128]{1,0:T(8,128)(2,1)S(1)}, u32[]{:S(2)}, u32[]{:S(2)}) collective-permute-start(bf16[64,128]{1,0:T(8,128)(2,1)S(1)} %get-tuple-element.25.kept), channel_id=1, source_target_pairs={{0,2},{1,3},{2,0},{3,1},{4,6},{5,7},{6,4},{7,5},{8,10},{9,11},{10,... | collective-permute-start | bytes 49160 | tf_op jit(solution)/shard_map/ppermute | solution.py:437
  14.2 3.3 %collective-permute-start.4 = (bf16[64,128]{1,0:T(8,128)(2,1)S(1)}, bf16[64,128]{1,0:T(8,128)(2,1)S(1)}, u32[]{:S(2)}, u32[]{:S(2)}) collective-permute-start(bf16[64,128]{1,0:T(8,128)(2,1)S(1)} %get-tuple-element.25.kept), channel_id=1, source_target_pairs={{0,4},{1,5},{2,6},{3,7},{4,0},{5,1},{6,2},{7,3},{8,12},{9,13},{10,... | collective-permute-start | bytes 49160 | tf_op jit(solution)/shard_map/ppermute | solution.py:437
  17.5 0.0 collective-permute-done.8.note_b
  17.5 1.6 %copy-done = bf16[512,2048]{1,0:T(8,128)(2,1)S(1)} copy-done((bf16[512,2048]{1,0:T(8,128)(2,1)S(1)}, bf16[512,2048]{1,0:T(8,128)(2,1)}, u32[]{:S(2)}) %copy-start) | copy-done | bytes 2097176
  19.1 0.9 copy-done.3
  20.0 4.7 %push.1 = (f32[512,128]{1,0:T(8,128)S(1)}, f32[512,128]{1,0:T(8,128)S(1)}) custom-call(bf16[64,2048]{1,0:T(8,128)(2,1)S(1)} %copy-done.3, bf16[512,2048]{1,0:T(8,128)(2,1)S(1)} %copy-done, bf16[80,256]{1,0:T(8,128)(2,1)S(1)} %collective-permute-done.8.note_b, bf16[80,256]{1,0:T(8,128)(2,1)S(1)} %collective-permute-done.9.note_a), custom_call_target="tpu_custom_call" | custom-call | tf_op jit(solution)/shard_map/push/pallas_call | solution.py:255
  24.8 1.9 %collective-permute-start.10 = (f32[512,128]{1,0:T(8,128)S(1)}, f32[512,128]{1,0:T(8,128)S(1)}, u32[]{:S(2)}, u32[]{:S(2)}) collective-permute-start(f32[512,128]{1,0:T(8,128)S(1)} %get-tuple-element.33), channel_id=1, source_target_pairs={{0,16},{16,32},{32,48},{48,64},{64,80},{80,96},{96,112},{112,128},... | collective-permute-start | bytes 786440 | tf_op jit(solution)/shard_map/ppermute | solution.py:490
  26.7 0.0 slice-start
  26.7 6.2 %collective-permute-start.11 = (f32[512,128]{1,0:T(8,128)S(1)}, f32[512,128]{1,0:T(8,128)S(1)}, u32[]{:S(2)}, u32[]{:S(2)}) collective-permute-start(f32[512,128]{1,0:T(8,128)S(1)} %get-tuple-element.34), channel_id=1, source_target_pairs={{16,0},{32,16},{48,32},{64,48},{80,64},{96,80},{112,96},{128,112},... | collective-permute-start | bytes 786440 | tf_op jit(solution)/shard_map/ppermute | solution.py:490
  32.9 0.0 copy-start.5
  32.9 0.1 slice.7
  33.0 0.0 copy-start.1
  33.0 2.2 %collective-permute-start.6 = (bf16[320,2048]{1,0:T(8,128)(2,1)S(1)}, bf16[320,2048]{1,0:T(8,128)(2,1)S(1)}, u32[]{:S(2)}, u32[]{:S(2)}) collective-permute-start(bf16[320,2048]{1,0:T(8,128)(2,1)S(1)} %slice.7), channel_id=1, source_target_pairs={{0,16},{16,32},{32,48},{48,64},{64,80},{80,96},{96,112},{112,128},... | collective-permute-start | bytes 3932168 | tf_op jit(solution)/shard_map/ppermute | solution.py:490
  35.2 0.0 collective-permute-done.3.o2
  35.2 6.0 %collective-permute-start.7 = (bf16[320,2048]{1,0:T(8,128)(2,1)S(1)}, bf16[320,2048]{1,0:T(8,128)(2,1)S(1)}, u32[]{:S(2)}, u32[]{:S(2)}) collective-permute-start(bf16[320,2048]{1,0:T(8,128)(2,1)S(1)} %slice.7), channel_id=1, source_target_pairs={{16,0},{32,16},{48,32},{64,48},{80,64},{96,80},{112,96},{128,112},... | collective-permute-start | bytes 3932168 | tf_op jit(solution)/shard_map/ppermute | solution.py:490
  41.3 0.0 collective-permute-done.4.o3
  41.3 4.6 %collective-permute-start.5 = (bf16[64,128]{1,0:T(8,128)(2,1)S(1)}, bf16[64,128]{1,0:T(8,128)(2,1)S(1)}, u32[]{:S(2)}, u32[]{:S(2)}) collective-permute-start(bf16[64,128]{1,0:T(8,128)(2,1)S(1)} %get-tuple-element.25.kept), channel_id=1, source_target_pairs={{0,8},{1,9},{2,10},{3,11},{4,12},{5,13},{6,14},{7,15},{8,0},{9,1},... | collective-permute-start | bytes 49160 | tf_op jit(solution)/shard_map/ppermute | solution.py:437
  45.9 0.1 pad_maximum_fusion
  46.0 3.0 %collective-permute-done.5.o4 = bf16[64,128]{1,0:T(8,128)(2,1)S(1)} collective-permute-done((bf16[64,128]{1,0:T(8,128)(2,1)S(1)}, bf16[64,128]{1,0:T(8,128)(2,1)S(1)}, u32[]{:S(2)}, u32[]{:S(2)}) %collective-permute-start.5) | collective-permute-done | bytes 16416 | tf_op jit(solution)/shard_map/ppermute | solution.py:437
  49.0 2.1 %collective-permute-start = (bf16[256,2048]{1,0:T(8,128)(2,1)S(1)}, bf16[256,2048]{1,0:T(8,128)(2,1)S(1)}, u32[]{:S(2)}, u32[]{:S(2)}) collective-permute-start(bf16[256,2048]{1,0:T(8,128)(2,1)S(1)} %pad_maximum_fusion), channel_id=1, source_target_pairs={{0,16},{16,32},{32,48},{48,64},{64,80},{80,96},{96,112},{112,128},... | collective-permute-start | bytes 3145736 | tf_op jit(solution)/shard_map/ppermute | solution.py:490
  51.1 6.9 %inverses.1 = (f32[512,128]{1,0:T(8,128)S(1)}, bf16[256,256]{1,0:T(8,128)(2,1)S(1)}, bf16[256,256]{1,0:T(8,128)(2,1)S(1)}, bf16[4,256,128]{2,1,0:T(8,128)(2,1)S(1)}, bf16[4,256,128]{2,1,0:T(8,128)(2,1)S(1)}) custom-call(bf16[64,2048]{1,0:T(8,128)(2,1)S(1)} %copy-done.3, bf16[512,2048]{1,0:T(8,128)(2,1)S(1)} %copy-done.1, bf16[512,2048]{1,0:T(8,128)(2,1)S(1)} %copy-done.5, ...), custom_call_target="tpu_custom_call" | custom-call | tf_op jit(solution)/shard_map/inverses/pallas_call | solution.py:221
  58.1 6.0 %collective-permute-start.1 = (bf16[256,2048]{1,0:T(8,128)(2,1)S(1)}, bf16[256,2048]{1,0:T(8,128)(2,1)S(1)}, u32[]{:S(2)}, u32[]{:S(2)}) collective-permute-start(bf16[256,2048]{1,0:T(8,128)(2,1)S(1)} %pad_maximum_fusion), channel_id=1, source_target_pairs={{16,0},{32,16},{48,32},{64,48},{80,64},{96,80},{112,96},{128,112},... | collective-permute-start | bytes 3145736 | tf_op jit(solution)/shard_map/ppermute | solution.py:490
  64.2 0.0 copy-start.4
  64.2 0.0 copy-start.7
  64.2 0.0 copy-start.9
  64.2 0.1 collective-permute-start.12
  64.3 1.5 %collective-permute-done.12.other = f32[512,128]{1,0:T(8,128)S(1)} collective-permute-done((f32[512,128]{1,0:T(8,128)S(1)}, f32[512,128]{1,0:T(8,128)S(1)}, u32[]{:S(2)}, u32[]{:S(2)}) %collective-permute-start.12) | collective-permute-done | bytes 262176 | tf_op jit(solution)/shard_map/ppermute | solution.py:437
  65.8 0.4 level_step.3.own.refs_4_
  66.2 2.0 %collective-permute-start.13 = (f32[512,128]{1,0:T(8,128)S(1)}, f32[512,128]{1,0:T(8,128)S(1)}, u32[]{:S(2)}, u32[]{:S(2)}) collective-permute-start(f32[512,128]{1,0:T(8,128)S(1)} %level_step.3.own.refs_4_), channel_id=1, source_target_pairs={{0,2},{2,0},{4,6},{6,4},{8,10},{10,8},{12,14},{14,12},{16,18},{18,... | collective-permute-start | bytes 786440 | tf_op jit(solution)/shard_map/ppermute | solution.py:437
  68.2 6.2 %collective-permute-done.13.other = f32[512,128]{1,0:T(8,128)S(1)} collective-permute-done((f32[512,128]{1,0:T(8,128)S(1)}, f32[512,128]{1,0:T(8,128)S(1)}, u32[]{:S(2)}, u32[]{:S(2)}) %collective-permute-start.13) | collective-permute-done | bytes 262176 | tf_op jit(solution)/shard_map/ppermute | solution.py:437
  74.5 0.4 level_step.4.own.refs_5_
  74.8 1.9 %collective-permute-start.14 = (f32[512,128]{1,0:T(8,128)S(1)}, f32[512,128]{1,0:T(8,128)S(1)}, u32[]{:S(2)}, u32[]{:S(2)}) collective-permute-start(f32[512,128]{1,0:T(8,128)S(1)} %level_step.4.own.refs_5_), channel_id=1, source_target_pairs={{0,4},{4,0},{8,12},{12,8},{16,20},{20,16},{24,28},{28,24},{32,36},... | collective-permute-start | bytes 786440 | tf_op jit(solution)/shard_map/ppermute | solution.py:437
  76.8 7.2 %collective-permute-done.14.other = f32[512,128]{1,0:T(8,128)S(1)} collective-permute-done((f32[512,128]{1,0:T(8,128)S(1)}, f32[512,128]{1,0:T(8,128)S(1)}, u32[]{:S(2)}, u32[]{:S(2)}) %collective-permute-start.14) | collective-permute-done | bytes 262176 | tf_op jit(solution)/shard_map/ppermute | solution.py:437
  84.0 0.4 level_step.5.refs_6_
  84.4 6.6 %collective-permute-start.15 = (f32[512,128]{1,0:T(8,128)S(1)}, f32[512,128]{1,0:T(8,128)S(1)}, u32[]{:S(2)}, u32[]{:S(2)}) collective-permute-start(f32[512,128]{1,0:T(8,128)S(1)} %level_step.5.refs_6_), channel_id=1, source_target_pairs={{0,8},{8,0},{16,24},{24,16},{32,40},{40,32},{48,56},{56,48},{64,72... | collective-permute-start | bytes 786440 | tf_op jit(solution)/shard_map/ppermute | solution.py:437
  91.0 5.3 %own_near.1 = (f32[512,2048]{1,0:T(8,128)S(1)}, bf16[256,2048]{1,0:T(8,128)(2,1)S(1)}, bf16[256,2048]{1,0:T(8,128)(2,1)S(1)}) custom-call(s32[4,4]{1,0:T(4,128)S(1)} %copy-done.7, s32[4]{0:T(128)S(1)} %copy-done.9, bf16[64,2048]{1,0:T(8,128)(2,1)S(1)} %copy-done.4, bf16[80,256]{1,0:T(8,128)(2,1)S(1)} %get-tuple-element.22.note, ...), custom_call_target="tpu_custom_call" | custom-call | tf_op jit(solution)/shard_map/own_near/pallas_call | solution.py:315
  96.4 2.6 %near_tiles.1.tiles = bf16[16,512,512]{2,1,0:T(8,128)(2,1)S(1)} custom-call(s32[4,4]{1,0:T(4,128)S(1)} %copy-done.7, s32[4]{0:T(128)S(1)} %copy-done.9, bf16[64,2048]{1,0:T(8,128)(2,1)S(1)} %copy-done.4, bf16[256,2048]{1,0:T(8,128)(2,1)S(1)} %collective-permute-done.before, bf16[256,2048]{1,0:T(8,128)(2,1)S(1)} %collective-permute-done.1.after), custom_call_target="tpu_custom_call" | custom-call | tf_op jit(solution)/shard_map/near_tiles/pallas_call | solution.py:360
  99.0 3.1 %near_part.2 = (f32[192,2048]{1,0:T(8,128)S(1)}, f32[192,256]{1,0:T(8,128)S(1)}) custom-call(s32[4,4]{1,0:T(4,128)S(1)} %copy-done.7, s32[4]{0:T(128)S(1)} %copy-done.9, f32[512,2048]{1,0:T(8,128)S(1)} %get-tuple-element.24.base, bf16[256,2048]{1,0:T(8,128)(2,1)S(1)} %collective-permute-done.before, bf16[256,2048]{1,0:T(8,128)(2,1)S(1)} %collective-permute-done.1.after, ...), custom_call_target="tpu_custom_call" | custom-call | tf_op jit(solution)/shard_map/near_part/pallas_call | solution.py:399
  102.1 3.8 %near_part.3 = (f32[320,2048]{1,0:T(8,128)S(1)}, f32[320,256]{1,0:T(8,128)S(1)}) custom-call(s32[4,4]{1,0:T(4,128)S(1)} %copy-done.7, s32[4]{0:T(128)S(1)} %copy-done.9, f32[512,2048]{1,0:T(8,128)S(1)} %get-tuple-element.24.base, bf16[320,2048]{1,0:T(8,128)(2,1)S(1)} %collective-permute-done.6.before, bf16[320,2048]{1,0:T(8,128)(2,1)S(1)} %collective-permute-done.7.after, ...), custom_call_target="tpu_custom_call" | custom-call | tf_op jit(solution)/shard_map/near_part/pallas_call | solution.py:399
  105.9 4.6 %finish.1 = f32[512,2048]{1,0:T(8,128)} custom-call(s32[4,4]{1,0:T(4,128)S(1)} %copy-done.7, f32[192,2048]{1,0:T(8,128)S(1)} %get-tuple-element.28.refs_0_, f32[192,256]{1,0:T(8,128)S(1)} %get-tuple-element.29.refs_1_, f32[320,2048]{1,0:T(8,128)S(1)} %get-tuple-element.30.refs_2_, f32[320,256]{1,0:T(8,128)S(1)} %get-tuple-element.31.refs_3_, ...), custom_call_target="tpu_custom_call" | custom-call | tf_op jit(solution)/shard_map/finish/pallas_call | solution.py:476
  (22 shorter events, 0.1 us)
Async XLA Ops:
  0.0 0.9 copy-start.2
  1.0 0.7 copy-start.6
  1.6 0.7 copy-start.8
  2.3 0.7 copy-start.10
  4.1 13.3 %collective-permute-start.8 = (bf16[80,256]{1,0:T(8,128)(2,1)S(1)}, bf16[80,256]{1,0:T(8,128)(2,1)S(1)}, u32[]{:S(2)}, u32[]{:S(2)}) collective-permute-start(bf16[80,256]{1,0:T(8,128)(2,1)S(1)} %get-tuple-element.22.note), channel_id=1, source_target_pairs={{0,16},{16,32},{32,48},{48,64},{64,80},{80,96},{96,112},{112,128},... | collective-permute-start | bytes 122888 | tf_op jit(solution)/shard_map/ppermute | solution.py:490
  7.6 9.9 %collective-permute-start.9 = (bf16[80,256]{1,0:T(8,128)(2,1)S(1)}, bf16[80,256]{1,0:T(8,128)(2,1)S(1)}, u32[]{:S(2)}, u32[]{:S(2)}) collective-permute-start(bf16[80,256]{1,0:T(8,128)(2,1)S(1)} %get-tuple-element.22.note), channel_id=1, source_target_pairs={{16,0},{32,16},{48,32},{64,48},{80,64},{96,80},{112,96},{128,112},... | collective-permute-start | bytes 122888 | tf_op jit(solution)/shard_map/ppermute | solution.py:490
  12.1 20.9 %collective-permute-start.2 = (bf16[64,128]{1,0:T(8,128)(2,1)S(1)}, bf16[64,128]{1,0:T(8,128)(2,1)S(1)}, u32[]{:S(2)}, u32[]{:S(2)}) collective-permute-start(bf16[64,128]{1,0:T(8,128)(2,1)S(1)} %get-tuple-element.25.kept), channel_id=1, source_target_pairs={{0,1},{1,0},{2,3},{3,2},{4,5},{5,4},{6,7},{7,6},{8,9},{9,8},{10,11... | collective-permute-start | bytes 49160 | tf_op jit(solution)/shard_map/ppermute | solution.py:437
  12.2 23.0 %collective-permute-start.3 = (bf16[64,128]{1,0:T(8,128)(2,1)S(1)}, bf16[64,128]{1,0:T(8,128)(2,1)S(1)}, u32[]{:S(2)}, u32[]{:S(2)}) collective-permute-start(bf16[64,128]{1,0:T(8,128)(2,1)S(1)} %get-tuple-element.25.kept), channel_id=1, source_target_pairs={{0,2},{1,3},{2,0},{3,1},{4,6},{5,7},{6,4},{7,5},{8,10},{9,11},{10,... | collective-permute-start | bytes 49160 | tf_op jit(solution)/shard_map/ppermute | solution.py:437
  14.2 27.1 %collective-permute-start.4 = (bf16[64,128]{1,0:T(8,128)(2,1)S(1)}, bf16[64,128]{1,0:T(8,128)(2,1)S(1)}, u32[]{:S(2)}, u32[]{:S(2)}) collective-permute-start(bf16[64,128]{1,0:T(8,128)(2,1)S(1)} %get-tuple-element.25.kept), channel_id=1, source_target_pairs={{0,4},{1,5},{2,6},{3,7},{4,0},{5,1},{6,2},{7,3},{8,12},{9,13},{10,... | collective-permute-start | bytes 49160 | tf_op jit(solution)/shard_map/ppermute | solution.py:437
  17.5 1.6 %copy-start = (bf16[512,2048]{1,0:T(8,128)(2,1)S(1)}, bf16[512,2048]{1,0:T(8,128)(2,1)}, u32[]{:S(2)}) copy-start(bf16[512,2048]{1,0:T(8,128)(2,1)} %w.5) | copy-start | bytes 6291460
  19.1 0.9 copy-start.3
  24.8 33.3 %collective-permute-start.10 = (f32[512,128]{1,0:T(8,128)S(1)}, f32[512,128]{1,0:T(8,128)S(1)}, u32[]{:S(2)}, u32[]{:S(2)}) collective-permute-start(f32[512,128]{1,0:T(8,128)S(1)} %get-tuple-element.33), channel_id=1, source_target_pairs={{0,16},{16,32},{32,48},{48,64},{64,80},{80,96},{96,112},{112,128},... | collective-permute-start | bytes 786440 | tf_op jit(solution)/shard_map/ppermute | solution.py:490
  26.7 19.1 %slice-start = ((bf16[512,2048]{1,0:T(8,128)(2,1)}), bf16[192,2048]{1,0:T(8,128)(2,1)S(1)}, s32[]{:S(2)}) async-start(bf16[512,2048]{1,0:T(8,128)(2,1)} %w.5), calls=%async_computation | async-start | bytes 1572864 | tf_op jit(solution)/shard_map/slice | solution.py:506
  26.7 37.4 %collective-permute-start.11 = (f32[512,128]{1,0:T(8,128)S(1)}, f32[512,128]{1,0:T(8,128)S(1)}, u32[]{:S(2)}, u32[]{:S(2)}) collective-permute-start(f32[512,128]{1,0:T(8,128)S(1)} %get-tuple-element.34), channel_id=1, source_target_pairs={{16,0},{32,16},{48,32},{64,48},{80,64},{96,80},{112,96},{128,112},... | collective-permute-start | bytes 786440 | tf_op jit(solution)/shard_map/ppermute | solution.py:490
  32.9 18.2 %copy-start.5 = (bf16[512,2048]{1,0:T(8,128)(2,1)S(1)}, bf16[512,2048]{1,0:T(8,128)(2,1)}, u32[]{:S(2)}) copy-start(bf16[512,2048]{1,0:T(8,128)(2,1)} %targets.3) | copy-start | bytes 6291460
  33.0 18.1 %copy-start.1 = (bf16[512,2048]{1,0:T(8,128)(2,1)S(1)}, bf16[512,2048]{1,0:T(8,128)(2,1)}, u32[]{:S(2)}) copy-start(bf16[512,2048]{1,0:T(8,128)(2,1)} %w.5) | copy-start | bytes 6291460
  33.0 69.1 %collective-permute-start.6 = (bf16[320,2048]{1,0:T(8,128)(2,1)S(1)}, bf16[320,2048]{1,0:T(8,128)(2,1)S(1)}, u32[]{:S(2)}, u32[]{:S(2)}) collective-permute-start(bf16[320,2048]{1,0:T(8,128)(2,1)S(1)} %slice.7), channel_id=1, source_target_pairs={{0,16},{16,32},{32,48},{48,64},{64,80},{80,96},{96,112},{112,128},... | collective-permute-start | bytes 3932168 | tf_op jit(solution)/shard_map/ppermute | solution.py:490
  35.2 66.9 %collective-permute-start.7 = (bf16[320,2048]{1,0:T(8,128)(2,1)S(1)}, bf16[320,2048]{1,0:T(8,128)(2,1)S(1)}, u32[]{:S(2)}, u32[]{:S(2)}) collective-permute-start(bf16[320,2048]{1,0:T(8,128)(2,1)S(1)} %slice.7), channel_id=1, source_target_pairs={{16,0},{32,16},{48,32},{64,48},{80,64},{96,80},{112,96},{128,112},... | collective-permute-start | bytes 3932168 | tf_op jit(solution)/shard_map/ppermute | solution.py:490
  41.3 7.7 %collective-permute-start.5 = (bf16[64,128]{1,0:T(8,128)(2,1)S(1)}, bf16[64,128]{1,0:T(8,128)(2,1)S(1)}, u32[]{:S(2)}, u32[]{:S(2)}) collective-permute-start(bf16[64,128]{1,0:T(8,128)(2,1)S(1)} %get-tuple-element.25.kept), channel_id=1, source_target_pairs={{0,8},{1,9},{2,10},{3,11},{4,12},{5,13},{6,14},{7,15},{8,0},{9,1},... | collective-permute-start | bytes 49160 | tf_op jit(solution)/shard_map/ppermute | solution.py:437
  49.0 47.4 %collective-permute-start = (bf16[256,2048]{1,0:T(8,128)(2,1)S(1)}, bf16[256,2048]{1,0:T(8,128)(2,1)S(1)}, u32[]{:S(2)}, u32[]{:S(2)}) collective-permute-start(bf16[256,2048]{1,0:T(8,128)(2,1)S(1)} %pad_maximum_fusion), channel_id=1, source_target_pairs={{0,16},{16,32},{32,48},{48,64},{64,80},{80,96},{96,112},{112,128},... | collective-permute-start | bytes 3145736 | tf_op jit(solution)/shard_map/ppermute | solution.py:490
  58.1 38.3 %collective-permute-start.1 = (bf16[256,2048]{1,0:T(8,128)(2,1)S(1)}, bf16[256,2048]{1,0:T(8,128)(2,1)S(1)}, u32[]{:S(2)}, u32[]{:S(2)}) collective-permute-start(bf16[256,2048]{1,0:T(8,128)(2,1)S(1)} %pad_maximum_fusion), channel_id=1, source_target_pairs={{16,0},{32,16},{48,32},{64,48},{80,64},{96,80},{112,96},{128,112},... | collective-permute-start | bytes 3145736 | tf_op jit(solution)/shard_map/ppermute | solution.py:490
  64.2 26.8 %copy-start.4 = (bf16[64,2048]{1,0:T(8,128)(2,1)S(1)}, bf16[64,2048]{1,0:T(8,128)(2,1)}, u32[]{:S(2)}) copy-start(bf16[64,2048]{1,0:T(8,128)(2,1)} %pts.7) | copy-start | bytes 786436
  64.2 26.8 %copy-start.7 = (s32[4,4]{1,0:T(4,128)S(1)}, s32[4,4]{1,0:T(4,128)}, u32[]{:S(2)}) copy-start(s32[4,4]{1,0:T(4,128)} %lists.9) | copy-start | bytes 196
  64.2 26.8 %copy-start.9 = (s32[4]{0:T(128)S(1)}, s32[4]{0:T(128)}, u32[]{:S(2)}) copy-start(s32[4]{0:T(128)} %counts.7) | copy-start | bytes 52
  64.2 1.6 %collective-permute-start.12 = (f32[512,128]{1,0:T(8,128)S(1)}, f32[512,128]{1,0:T(8,128)S(1)}, u32[]{:S(2)}, u32[]{:S(2)}) collective-permute-start(f32[512,128]{1,0:T(8,128)S(1)} %join.1.own), channel_id=1, source_target_pairs={{0,1},{1,0},{2,3},{3,2},{4,5},{5,4},{6,7},{7,6},{8,9},{9,8},{10,11... | collective-permute-start | bytes 786440 | tf_op jit(solution)/shard_map/ppermute | solution.py:437
  66.2 8.3 %collective-permute-start.13 = (f32[512,128]{1,0:T(8,128)S(1)}, f32[512,128]{1,0:T(8,128)S(1)}, u32[]{:S(2)}, u32[]{:S(2)}) collective-permute-start(f32[512,128]{1,0:T(8,128)S(1)} %level_step.3.own.refs_4_), channel_id=1, source_target_pairs={{0,2},{2,0},{4,6},{6,4},{8,10},{10,8},{12,14},{14,12},{16,18},{18,... | collective-permute-start | bytes 786440 | tf_op jit(solution)/shard_map/ppermute | solution.py:437
  74.8 9.2 %collective-permute-start.14 = (f32[512,128]{1,0:T(8,128)S(1)}, f32[512,128]{1,0:T(8,128)S(1)}, u32[]{:S(2)}, u32[]{:S(2)}) collective-permute-start(f32[512,128]{1,0:T(8,128)S(1)} %level_step.4.own.refs_5_), channel_id=1, source_target_pairs={{0,4},{4,0},{8,12},{12,8},{16,20},{20,16},{24,28},{28,24},{32,36},... | collective-permute-start | bytes 786440 | tf_op jit(solution)/shard_map/ppermute | solution.py:437
  84.4 21.6 %collective-permute-start.15 = (f32[512,128]{1,0:T(8,128)S(1)}, f32[512,128]{1,0:T(8,128)S(1)}, u32[]{:S(2)}, u32[]{:S(2)}) collective-permute-start(f32[512,128]{1,0:T(8,128)S(1)} %level_step.5.refs_6_), channel_id=1, source_target_pairs={{0,8},{8,0},{16,24},{24,16},{32,40},{40,32},{48,56},{56,48},{64,72... | collective-permute-start | bytes 786440 | tf_op jit(solution)/shard_map/ppermute | solution.py:437
where the time goes:
time: 113 us; the launch traced here: 111 us
  starting transfers between devices  53 us (47%)
  Pallas kernels  33.4 us (30%)
  waiting for transfers between devices  18.1 us (16%)
  local copies, waits for them, and re-layouts  5.63 us (5%)
    ppermute x8, starting transfers between devices, shifted(): return lax.ppermute(value, 'clus', pairs)  32.4 us
    ppermute x8, starting transfers between devices, among_leaves(): return lax.ppermute(value, 'leaf', pairs)  20.6 us
    ppermute x8, waiting for transfers between devices, among_leaves(): return lax.ppermute(value, 'leaf', pairs)  18 us
    pallas_call x1, Pallas kernels, inverses(): pl.pallas_call(inverse_kernel, out_shape=(jax.ShapeDtypeStruct((rows, hal...  6.93 us
    pallas_call x2, Pallas kernels, near_part(): pl.pallas_call(functools.partial(near_kernel, first, skip), out_shape=(ja...  6.93 us
    unnamed x22, local copies, waits for them, and re-layouts  5.53 us
    pallas_call x1, Pallas kernels, own_near(): pl.pallas_call(own_kernel, out_shape=(jax.ShapeDtypeStruct(weights.shape,...  5.33 us
    pallas_call x1, Pallas kernels, push(): pl.pallas_call(push_kernel, out_shape=(jax.ShapeDtypeStruct((rows, s // 2...  4.74 us
  transfers between devices with their start and end apart: 16, of which 4 were waited for; matrix products, arithmetic and copies ran while one was open for 0% of the time, Pallas kernels for 25%

commit v1 on v0

--- a/solution.py
+++ b/solution.py
@@ -12,7 +12,7 @@
 N_LEAF = 16
 RIDGE = 0.5
 SHIFT = 4.0
-EARLY_ROWS = 192
+EARLY_ROWS = 224
 COARSE_STEPS = 4
 FINE_STEPS = 2
 
@@ -66,13 +66,13 @@
 
 
 def prep_kernel(*refs):
-    srcs, (pick, note, kept), dsts, sems = refs[:4], refs[4:7], refs[7:11], refs[11]
+    srcs, (pick, note, kept), dsts, sems = refs[:3], refs[3:6], refs[6:9], refs[9]
     copies = [pltpu.make_async_copy(a, b, sems.at[k]) for k, (a, b) in enumerate(zip(srcs, dsts))]
     for copy in copies:
         copy.start()
     for copy in copies:
         copy.wait()
-    lists, counts, pts, skel = dsts
+    lists, pts, skel = dsts
     features, n = pts.shape
     s = skel.shape[1]
     clusters, slots = lists.shape
@@ -91,12 +91,12 @@
             listed = lists[g, slot]
             way = listed // clusters - lists[0, 0] // clusters
             begin = jnp.where(way < 0, 0, jnp.where(way > 0, clusters, 2 * clusters))
-            at = jnp.where(slot < counts[g], begin + listed % clusters, -1)
+            at = jnp.where(is_live(lists, g, slot), begin + listed % clusters, -1)
             flags = jnp.where((line == at) & (home == g), 1.0, flags)
     note[features:, :] = flags.astype(bf16)
 
 
-def prep(near_lists, tile_counts, points, skeleton):
+def prep(near_lists, points, skeleton):
     features, n = points.shape
     s = skeleton.shape[1]
     return pl.pallas_call(
@@ -106,21 +106,20 @@
             jax.ShapeDtypeStruct((features + 16, s), bf16),
             jax.ShapeDtypeStruct((features, s // 2), bf16),
         ),
-        in_specs=[pl.BlockSpec(memory_space=pltpu.HBM)] * 4,
+        in_specs=[pl.BlockSpec(memory_space=pltpu.HBM)] * 3,
         out_specs=(VMEM, VMEM, VMEM),
         scratch_shapes=[
             pltpu.SMEM(near_lists.shape, jnp.int32),
-            pltpu.SMEM(tile_counts.shape, jnp.int32),
             pltpu.VMEM(points.shape, bf16),
             pltpu.VMEM(skeleton.shape, jnp.int32),
-            pltpu.SemaphoreType.DMA((4,)),
+            pltpu.SemaphoreType.DMA((3,)),
         ],
-        compiler_params=params(),
+        compiler_params=params(60),
         name="prep",
-    )(near_lists, tile_counts, points, skeleton)
-
-
-def invert(grams, between=()):
+    )(near_lists, points, skeleton)
+
+
+def invert(grams, between=(), whole=0):
     between = list(between)
     share = -(-len(between) // (COARSE_STEPS + FINE_STEPS))
 
@@ -147,21 +146,24 @@
         gaps.append(0.5 * gain * gap * gap)
     for _ in range(COARSE_STEPS):
         lows = [x.astype(bf16) for x in guesses]
-        prods = [mm(gh, x) + mm(gl, x) for (gh, gl), x in zip(parts, lows)]
+        prods = [mm(gh, x) for (gh, _), x in zip(parts, lows)]
         work()
         gains = [2.0 / (2.0 - gap * gap) for gap in gaps]
         guesses = [
             gain * mm(x, (2.0 * eye - p).astype(bf16)) for gain, x, p in zip(gains, lows, prods)
         ]
         gaps = [0.5 * gain * gap * gap for gain, gap in zip(gains, gaps)]
-    for _ in range(FINE_STEPS):
+    for step in range(FINE_STEPS):
         splits = [split(x) for x in guesses]
+        wide = [s if step < FINE_STEPS - 1 or k < whole else s // 2 for k in range(len(grams))]
         prods = [
-            mm(gh, xh) + (mm(gh, xl) + mm(gl, xh)) for (gh, gl), (xh, xl) in zip(parts, splits)
+            mm(gh, xh[:, :c]) + (mm(gh, xl[:, :c]) + mm(gl, xh[:, :c]))
+            for (gh, gl), (xh, xl), c in zip(parts, splits, wide)
         ]
         work()
         guesses = [
-            x + mm(xh, (eye - p).astype(bf16)) for x, (xh, _), p in zip(guesses, splits, prods)
+            x[:, :c] + mm(xh, (eye[:, :c] - p).astype(bf16))
+            for x, (xh, _), p, c in zip(guesses, splits, prods, wide)
         ]
     while between:
         between.pop(0)()
@@ -185,7 +187,7 @@
     return mm(vh, high) + (mm(vh, low) + mm(vl, high))
 
 
-def inverse_kernel(pts, w, targets, pick, note, kept, o1, o2, o3, o4, mine, a_high, a_low, b_high, b_low, left, total):
+def inverse_kernel(pts, w, targets, pick, note, kept, o1, o2, o3, o4, from_b, from_a, start, a_high, a_low, b_high, b_low, left, total):
     features, half = kept.shape
     clusters = pts.shape[1] // CLUSTER_PTS
     left[...] = lifted(pts[...])[0]
@@ -203,15 +205,15 @@
     def rest():
         total[...] = mm(targets[...], pick[...]) - RIDGE * mm(w[...], pick[...]) - total[...]
 
-    found = invert(grams, jobs + [rest])
+    found = invert(grams, jobs + [rest], 1)
     ah, al = split(found[0])
     a_high[...], a_low[...] = ah, al
     for k in range(4):
-        b_high[k], b_low[k] = split(SHIFT * found[k + 1][:, :half])
-    mine[...] = solve_rows(total[...], ah[:, :half], al[:, :half])
-
-
-def inverses(points, weights, targets, pick, note, kept, others):
+        b_high[k], b_low[k] = split(SHIFT * found[k + 1])
+    start[...] = solve_rows(total[...], ah[:, :half], al[:, :half]) - from_b[...] - from_a[...]
+
+
+def inverses(points, weights, targets, pick, note, kept, others, from_b, from_a):
     features, n = points.shape
     rows = weights.shape[0]
     half = kept.shape[1]
@@ -221,17 +223,16 @@
     return pl.pallas_call(
         inverse_kernel,
         out_shape=(jax.ShapeDtypeStruct((rows, half), f32), full, full, part, part),
-        in_specs=[VMEM] * 10,
+        in_specs=[VMEM] * 12,
         out_specs=(VMEM,) * 5,
         scratch_shapes=[pltpu.VMEM((features + 16, n), bf16), pltpu.VMEM((rows, s), f32)],
         compiler_params=params(),
         name="inverses",
-    )(points, weights, targets, pick, note, kept, *others)
+    )(points, weights, targets, pick, note, kept, *others, from_b, from_a)
 
 
 def push_kernel(pts, w, note_b, note_a, to_b, to_a, left, total):
     features, n = pts.shape
-    half = to_b.shape[1]
     clusters = n // CLUSTER_PTS
     left[...] = lifted(pts[...])[0]
     notes = ((note_b, clusters), (note_a, 0))
@@ -244,7 +245,7 @@
             for j in range(clusters)
         ]
     for k, found in enumerate(invert(grams, jobs)):
-        high, low = split(found[:, :half])
+        high, low = split(found)
         (to_b, to_a)[k][...] = solve_rows(total[k], high, low)
 
 
@@ -263,22 +264,11 @@
     )(points, weights, note_b, note_a)
 
 
-def join_kernel(mine, from_b, from_a, out):
-    out[...] = mine[...] - from_b[...] - from_a[...]
-
-
-def join(mine, from_b, from_a):
-    return pl.pallas_call(
-        join_kernel,
-        out_shape=jax.ShapeDtypeStruct(mine.shape, f32),
-        in_specs=[VMEM] * 3,
-        out_specs=VMEM,
-        compiler_params=params(),
-        name="join",
-    )(mine, from_b, from_a)
-
-
-def pair_of(lists, counts, i):
+def is_live(lists, g, slot):
+    return (slot == 0) | (lists[g, slot] != lists[g, 0])
+
+
+def pair_of(lists, i):
     slots = lists.shape[1]
     clusters = lists.shape[0]
     g = i // slots
@@ -286,19 +276,16 @@
     way = listed // clusters - lists[0, 0] // clusters
     cols = pl.multiple_of((listed % clusters) * CLUSTER_PTS, CLUSTER_PTS)
     own_cols = pl.multiple_of(g * CLUSTER_PTS, CLUSTER_PTS)
-    return (i % slots) < counts[g], way, pl.ds(cols, CLUSTER_PTS), pl.ds(own_cols, CLUSTER_PTS)
-
-
-def own_kernel(lists, counts, pts, note, w, targets, pick, out, spread_tile, place, left, right, tile):
+    return is_live(lists, g, i % slots), way, pl.ds(cols, CLUSTER_PTS), pl.ds(own_cols, CLUSTER_PTS)
+
+
+def own_kernel(lists, pts, w, targets, out, left, right, tile):
     features = pts.shape[0]
     left[...], right[...] = lifted(pts[...])
-    node_left = lifted(note[:features, :])[0]
-    spread_tile[...] = kernel_of(node_left, right[...], features).astype(bf16)
-    place[...] = pick[...].T
     out[...] = targets[...].astype(f32) - RIDGE * w[...].astype(f32)
 
     def step(i, carry):
-        live, way, cols, own = pair_of(lists, counts, i)
+        live, way, cols, own = pair_of(lists, i)
 
         @pl.when(live & (way == 0))
         def _():
@@ -310,17 +297,13 @@
     lax.fori_loop(0, lists.shape[0] * lists.shape[1], step, 0)
 
 
-def own_near(points, note, weights, targets, pick, near_lists, tile_counts):
+def own_near(points, weights, targets, near_lists):
     features, n = points.shape
     return pl.pallas_call(
         own_kernel,
-        out_shape=(
-            jax.ShapeDtypeStruct(weights.shape, f32),
-            jax.ShapeDtypeStruct((note.shape[1], n), bf16),
-            jax.ShapeDtypeStruct((note.shape[1], n), bf16),
-        ),
-        in_specs=[SMEM, SMEM] + [VMEM] * 5,
-        out_specs=(VMEM, VMEM, VMEM),
+        out_shape=jax.ShapeDtypeStruct(weights.shape, f32),
+        in_specs=[SMEM] + [VMEM] * 3,
+        out_specs=VMEM,
         scratch_shapes=[
             pltpu.VMEM((features + 16, n), bf16),
             pltpu.VMEM((features + 16, n), bf16),
@@ -328,17 +311,36 @@
         ],
         compiler_params=params(),
         name="own_near",
-    )(near_lists, tile_counts, points, note, weights, targets, pick)
-
-
-def tiles_kernel(lists, counts, pts, before, after, out, lb, la, right):
+    )(near_lists, points, weights, targets)
+
+
+def tables_kernel(pts, note, pick, spread_tile, place):
+    features = pts.shape[0]
+    node_left = lifted(note[:features, :])[0]
+    spread_tile[...] = kernel_of(node_left, lifted(pts[...])[1], features).astype(bf16)
+    place[...] = pick[...].T
+
+
+def tables(points, note, pick):
+    shape = jax.ShapeDtypeStruct((note.shape[1], points.shape[1]), bf16)
+    return pl.pallas_call(
+        tables_kernel,
+        out_shape=(shape, shape),
+        in_specs=[VMEM] * 3,
+        out_specs=(VMEM, VMEM),
+        compiler_params=params(),
+        name="tables",
+    )(points, note, pick)
+
+
+def tiles_kernel(lists, pts, before, after, out, lb, la, right):
     features = pts.shape[0]
     right[...] = lifted(pts[...])[1]
     lb[...] = lifted(before[...])[0]
     la[...] = lifted(after[...])[0]
 
     def step(i, carry):
-        live, way, cols, own = pair_of(lists, counts, i)
+        live, way, cols, own = pair_of(lists, i)
 
         @pl.when(live & (way < 0))
         def _():
@@ -353,7 +355,7 @@
     lax.fori_loop(0, lists.shape[0] * lists.shape[1], step, 0)
 
 
-def near_tiles(points, before, after, near_lists, tile_counts):
+def near_tiles(points, before, after, near_lists):
     features, n = points.shape
     pairs = near_lists.shape[0] * near_lists.shape[1]
     head = pl.BlockSpec((features, n), lambda i: (0, 0))
@@ -361,20 +363,20 @@
         tiles_kernel,
         out_shape=jax.ShapeDtypeStruct((pairs, CLUSTER_PTS, CLUSTER_PTS), bf16),
         grid=(1,),
-        in_specs=[SMEM, SMEM, VMEM, head, head],
+        in_specs=[SMEM, VMEM, head, head],
         out_specs=VMEM,
         scratch_shapes=[pltpu.VMEM((features + 16, n), bf16)] * 3,
         compiler_params=params(),
         name="near_tiles",
-    )(near_lists, tile_counts, points, before, after)
-
-
-def near_kernel(first, skip, lists, counts, base, before, after, tiles, pick, a_high, a_low, res, sol):
+    )(near_lists, points, before, after)
+
+
+def near_kernel(first, skip, lists, base, before, after, tiles, pick, a_high, a_low, res, sol):
     rows = res.shape[0]
     res[...] = base[first : first + rows, :]
 
     def step(i, carry):
-        live, way, cols, own = pair_of(lists, counts, i)
+        live, way, cols, own = pair_of(lists, i)
 
         @pl.when(live & (way < 0))
         def _():
@@ -393,27 +395,30 @@
     sol[...] = both[:rows] + (mm(node[:rows], a_low[...]) + both[rows:])
 
 
-def near_part(first, rows, skip, base, before, after, tiles, pick, a_high, a_low, near_lists, tile_counts):
+def near_part(first, rows, skip, base, before, after, tiles, pick, a_high, a_low, near_lists):
     n = base.shape[1]
     s = pick.shape[1]
     return pl.pallas_call(
         functools.partial(near_kernel, first, skip),
         out_shape=(jax.ShapeDtypeStruct((rows, n), f32), jax.ShapeDtypeStruct((rows, s), f32)),
-        in_specs=[SMEM, SMEM] + [VMEM] * 7,
+        in_specs=[SMEM] + [VMEM] * 7,
         out_specs=(VMEM, VMEM),
         compiler_params=params(),
         name="near_part",
-    )(near_lists, tile_counts, base, before, after, tiles, pick, a_high, a_low)
+    )(near_lists, base, before, after, tiles, pick, a_high, a_low)
 
 
 def joint(own, other, b_high, b_low, at):
     half = own.shape[1]
     total = None
     for begin, piece in ((0, own), (half, other)):
-        high, low = split(piece[...])
         bh = b_high[at, begin : begin + half, :]
         bl = b_low[at, begin : begin + half, :]
-        term = mm(high, bh) + (mm(high, bl) + mm(low, bh))
+        if piece.dtype == bf16:
+            term = mm(piece[...], bh) + mm(piece[...], bl)
+        else:
+            high, low = split(piece[...])
+            term = mm(high, bh) + (mm(high, bl) + mm(low, bh))
         total = term if total is None else total + term
     return total
 
@@ -437,51 +442,72 @@
     return lax.ppermute(value, "leaf", pairs)
 
 
-def out_kernel(cuts, lists, *refs):
+def settle_kernel(cuts, lists, *refs):
     parts = refs[: 2 * len(cuts)]
-    v1, v2, v3, w4, b_high, b_low, tile, place, out, buf, sems = refs[2 * len(cuts) :]
+    v1, v2, v3, place, ready, corr = refs[2 * len(cuts) :]
     half = v1.shape[1]
     leaf = leaf_of(lists)
-    inject = v1[...]
-    inject = inject + jnp.where(leaf % 2 == 0, v2[...], 0.0)
-    inject = inject + jnp.where(leaf % 4 == 0, v3[...], 0.0)
-    inject = inject + jnp.where(leaf % 8 == 0, joint(v3, w4, b_high, b_low, 3), 0.0)
+    at = 0
+    for k, rows in enumerate(cuts):
+        res, sol = parts[2 * k : 2 * k + 2]
+        here = slice(at, at + rows)
+        inject = v1[here, :] + jnp.where(leaf % 2 == 0, v2[here, :], 0.0)
+        inject = inject + jnp.where(leaf % 4 == 0, v3[here, :], 0.0)
+        corr[here, :half] = sol[:, :half] + inject
+        corr[here, half:] = sol[:, half:]
+        high, low = split(corr[here, :])
+        ready[here, :] = res[...] * (1.0 / (1.0 + RIDGE)) + mm(high, place[...]) + mm(low, place[...])
+        at += rows
+
+
+def settle(cuts, near_lists, parts, rest):
+    total = sum(cuts)
+    n = parts[0].shape[1]
+    return pl.pallas_call(
+        functools.partial(settle_kernel, cuts),
+        out_shape=(
+            jax.ShapeDtypeStruct((total, n), f32),
+            jax.ShapeDtypeStruct((total, parts[1].shape[1]), f32),
+        ),
+        in_specs=[SMEM] + [VMEM] * (len(parts) + len(rest)),
+        out_specs=(VMEM, VMEM),
+        compiler_params=params(),
+        name="settle",
+    )(near_lists, *parts, *rest)
+
+
+def out_kernel(blocks, lists, ready, corr, v3, w4, b_high, b_low, tile, place, out, buf, sems):
+    half = v3.shape[1]
+    leaf = leaf_of(lists)
+    last = jnp.where(leaf % 8 == 0, joint(v3, w4, b_high, b_low, 3), 0.0)
+    last_high, last_low = split(last)
+    twice = jnp.concatenate([place[:half, :], place[:half, :]], axis=0)
     copies = []
     at = 0
-    for k, blocks in enumerate(cuts):
-        res, sol = parts[2 * k : 2 * k + 2]
-        inner = 0
-        for rows in blocks:
-            solved = sol[inner : inner + rows, :]
-            corr = jnp.concatenate([solved[:, :half] + inject[at : at + rows], solved[:, half:]], axis=1)
-            high, low = split(corr)
-            spread = mm(high, tile[...])
-            spread = spread + mm(high, place[...]) + mm(low, place[...])
-            buf[at : at + rows, :] = res[inner : inner + rows, :] * (1.0 / (1.0 + RIDGE)) + spread
-            copy = pltpu.make_async_copy(
-                buf.at[pl.ds(at, rows)], out.at[pl.ds(at, rows)], sems.at[len(copies)]
-            )
-            copy.start()
-            copies.append(copy)
-            at += rows
-            inner += rows
+    for k, rows in enumerate(blocks):
+        here = slice(at, at + rows)
+        full = jnp.concatenate([corr[here, :half] + last[here], corr[here, half:]], axis=1)
+        added = jnp.concatenate([last_high[here], last_low[here]], axis=1)
+        buf[here, :] = ready[here, :] + mm(full.astype(bf16), tile[...]) + mm(added, twice)
+        copy = pltpu.make_async_copy(buf.at[pl.ds(at, rows)], out.at[pl.ds(at, rows)], sems.at[k])
+        copy.start()
+        copies.append(copy)
+        at += rows
     for copy in copies:
         copy.wait()
 
 
-def finish(cuts, near_lists, parts, rest):
-    total = sum(sum(blocks) for blocks in cuts)
-    count = sum(len(blocks) for blocks in cuts)
-    n = parts[0].shape[1]
-    return pl.pallas_call(
-        functools.partial(out_kernel, cuts),
+def finish(blocks, near_lists, *args):
+    total, n = args[0].shape
+    return pl.pallas_call(
+        functools.partial(out_kernel, blocks),
         out_shape=jax.ShapeDtypeStruct((total, n), f32),
-        in_specs=[SMEM] + [VMEM] * (len(parts) + len(rest)),
+        in_specs=[SMEM] + [VMEM] * len(args),
         out_specs=pl.BlockSpec(memory_space=pl.ANY),
-        scratch_shapes=[pltpu.VMEM((total, n), f32), pltpu.SemaphoreType.DMA((count,))],
+        scratch_shapes=[pltpu.VMEM((total, n), f32), pltpu.SemaphoreType.DMA((len(blocks),))],
         compiler_params=params(),
         name="finish",
-    )(near_lists, *parts, *rest)
+    )(near_lists, *args)
 
 
 def shifted(value, by):
@@ -501,7 +527,7 @@
     size = lax.axis_size("leaf")
     steps = [[(i, i ^ (1 << k)) for i in range(0, size, 1 << k)] for k in range(4)]
 
-    pick, note, kept = prep(near_lists, tile_counts, points, skeleton)
+    pick, note, kept = prep(near_lists, points, skeleton)
     note_b, note_a = both_ways(note)
     first = jnp.concatenate([points, weights[:EARLY_ROWS]], axis=0)
     before_1, after_1 = both_ways(first)
@@ -512,25 +538,26 @@
     before_2, after_2 = both_ways(second)
     swaps = [[(i, i ^ (1 << k)) for i in range(size)] for k in range(4)]
     others = [among_leaves(kept, swaps[k]) for k in range(4)]
-    mine, a_high, a_low, b_high, b_low = inverses(
-        points, weights, targets, pick, note, kept, others
+    v0, a_high, a_low, b_high, b_low = inverses(
+        points, weights, targets, pick, note, kept, others, from_b, from_a
     )
-    v0 = join(mine, from_b, from_a)
-
-    base, tile, place = own_near(points, note, weights, targets, pick, near_lists, tile_counts)
-    tiles = near_tiles(points, before_1, after_1, near_lists, tile_counts)
-    shared = (tiles, pick, a_high, a_low, near_lists, tile_counts)
+
+    base = own_near(points, weights, targets, near_lists)
+    tiles = near_tiles(points, before_1, after_1, near_lists)
+    shared = (tiles, pick, a_high, a_low, near_lists)
     res_1, sol_1 = near_part(0, EARLY_ROWS, features, base, before_1, after_1, *shared)
     res_2, sol_2 = near_part(EARLY_ROWS, late, 0, base, before_2, after_2, *shared)
 
+    tile, place = tables(points, note, pick)
+
     v1 = level_step(0, v0, among_leaves(v0, steps[0]), b_high, b_low)
-    v2 = level_step(1, v1, among_leaves(v1, steps[1]), b_high, b_low)
-    v3 = level_step(2, v2, among_leaves(v2, steps[2]), b_high, b_low)
-    w4 = among_leaves(v3, steps[3])
-    cuts = ((EARLY_ROWS,), (late // 2, late // 2))
-    return finish(
-        cuts, near_lists, (res_1, sol_1, res_2, sol_2), (v1, v2, v3, w4, b_high, b_low, tile, place)
+    v2 = level_step(1, v1, among_leaves(v1.astype(bf16), steps[1]), b_high, b_low)
+    v3 = level_step(2, v2, among_leaves(v2.astype(bf16), steps[2]), b_high, b_low)
+    w4 = among_leaves(v3.astype(bf16), steps[3])
+    ready, corr = settle(
+        (EARLY_ROWS, late), near_lists, (res_1, sol_1, res_2, sol_2), (v1, v2, v3, place)
     )
+    return finish((192, 192, 128), near_lists, ready, corr, v3, w4, b_high, b_low, tile, place)
 
 
 def solution(mesh):

time: 113 us -> 145 us (1.28)
  the two profiles are of different devices: /device:TPU:6 before, /device:TPU:10 now
where the time goes in v1:
time: 145 us
  waiting for transfers between devices  58.2 us (40%)
  starting transfers between devices  47.5 us (33%)
  Pallas kernels  38.3 us (26%)
    ppermute x8, waiting for transfers between devices, shifted(): return lax.ppermute(value, 'clus', pairs)  48.3 us
    ppermute x8, starting transfers between devices, shifted(): return lax.ppermute(value, 'clus', pairs)  27.8 us
    ppermute x8, starting transfers between devices, among_leaves(): return lax.ppermute(value, 'leaf', pairs)  19.8 us
    ppermute x8, waiting for transfers between devices, among_leaves(): return lax.ppermute(value, 'leaf', pairs)  9.87 us
    pallas_call x2, Pallas kernels, near_part(): pl.pallas_call(functools.partial(near_kernel, first, skip), out_shape=(ja...  7.58 us
    pallas_call x1, Pallas kernels, own_near(): pl.pallas_call(own_kernel, out_shape=jax.ShapeDtypeStruct(weights.shape,...  6.84 us
    pallas_call x1, Pallas kernels, inverses(): pl.pallas_call(inverse_kernel, out_shape=(jax.ShapeDtypeStruct((rows, hal...  6.6 us
    pallas_call x1, Pallas kernels, push(): pl.pallas_call(push_kernel, out_shape=(jax.ShapeDtypeStruct((rows, s // 2...  4.59 us
  transfers between devices with their start and end apart: 16, of which 5 were waited for; matrix products, arithmetic and copies ran while one was open for 0% of the time, Pallas kernels for 22%

profile of v1, /device:TPU:10, one launch (start us, length us, event | category | flops | bytes accessed | tf_op | source)
XLA Modules:
  0.0 144.9 jit_solution(2758791894690715085)
XLA Ops:
  0.0 2.4 %prep.1 = (bf16[2048,256]{1,0:T(8,128)(2,1)}, bf16[80,256]{1,0:T(8,128)(2,1)}, bf16[64,128]{1,0:T(8,128)(2,1)}) custom-call(s32[4,4]{1,0:T(4,128)} %lists.11, bf16[64,2048]{1,0:T(8,128)(2,1)} %pts.9, s32[1,256]{1,0:T(1,128)} %refs_2_.1), custom_call_target="tpu_custom_call" | custom-call | tf_op jit(solution)/shard_map/prep/pallas_call | solution.py:102
  2.4 3.5 %collective-permute-start.6 = (bf16[80,256]{1,0:T(8,128)(2,1)}, bf16[80,256]{1,0:T(8,128)(2,1)S(1)}, u32[]{:S(2)}, u32[]{:S(2)}) collective-permute-start(bf16[80,256]{1,0:T(8,128)(2,1)} %get-tuple-element.24.note), channel_id=1, source_target_pairs={{0,16},{16,32},{32,48},{48,64},{64,80},{80,96},{96,112},{112,128},... | collective-permute-start | bytes 122888 | tf_op jit(solution)/shard_map/ppermute | solution.py:516
  5.9 0.0 copy-start
  5.9 0.1 collective-permute-start.2
  6.0 2.0 %collective-permute-start.3 = (bf16[64,128]{1,0:T(8,128)(2,1)}, bf16[64,128]{1,0:T(8,128)(2,1)S(1)}, u32[]{:S(2)}, u32[]{:S(2)}) collective-permute-start(bf16[64,128]{1,0:T(8,128)(2,1)} %get-tuple-element.25.kept), channel_id=1, source_target_pairs={{0,2},{1,3},{2,0},{3,1},{4,6},{5,7},{6,4},{7,5},{8,10},{9,11},{10,... | collective-permute-start | bytes 49160 | tf_op jit(solution)/shard_map/ppermute | solution.py:442
  8.0 3.3 %collective-permute-start.4 = (bf16[64,128]{1,0:T(8,128)(2,1)}, bf16[64,128]{1,0:T(8,128)(2,1)S(1)}, u32[]{:S(2)}, u32[]{:S(2)}) collective-permute-start(bf16[64,128]{1,0:T(8,128)(2,1)} %get-tuple-element.25.kept), channel_id=1, source_target_pairs={{0,4},{1,5},{2,6},{3,7},{4,0},{5,1},{6,2},{7,3},{8,12},{9,13},{10,... | collective-permute-start | bytes 49160 | tf_op jit(solution)/shard_map/ppermute | solution.py:442
  11.3 4.5 %collective-permute-start.5 = (bf16[64,128]{1,0:T(8,128)(2,1)}, bf16[64,128]{1,0:T(8,128)(2,1)S(1)}, u32[]{:S(2)}, u32[]{:S(2)}) collective-permute-start(bf16[64,128]{1,0:T(8,128)(2,1)} %get-tuple-element.25.kept), channel_id=1, source_target_pairs={{0,8},{1,9},{2,10},{3,11},{4,12},{5,13},{6,14},{7,15},{8,0},{9,1},... | collective-permute-start | bytes 49160 | tf_op jit(solution)/shard_map/ppermute | solution.py:442
  15.8 2.3 %collective-permute-start.7 = (bf16[80,256]{1,0:T(8,128)(2,1)}, bf16[80,256]{1,0:T(8,128)(2,1)S(1)}, u32[]{:S(2)}, u32[]{:S(2)}) collective-permute-start(bf16[80,256]{1,0:T(8,128)(2,1)} %get-tuple-element.24.note), channel_id=1, source_target_pairs={{16,0},{32,16},{48,32},{64,48},{80,64},{96,80},{112,96},{128,112},... | collective-permute-start | bytes 122888 | tf_op jit(solution)/shard_map/ppermute | solution.py:516
  18.2 0.1 pad_maximum_fusion
  18.3 0.0 copy-start.1
  18.3 0.0 copy-start.3
  18.4 3.6 %collective-permute-done.7.note_a = bf16[80,256]{1,0:T(8,128)(2,1)S(1)} collective-permute-done((bf16[80,256]{1,0:T(8,128)(2,1)}, bf16[80,256]{1,0:T(8,128)(2,1)S(1)}, u32[]{:S(2)}, u32[]{:S(2)}) %collective-permute-start.7) | collective-permute-done | bytes 40992 | tf_op jit(solution)/shard_map/ppermute | solution.py:516
  21.9 4.6 %push.1 = (f32[512,128]{1,0:T(8,128)S(1)}, f32[512,128]{1,0:T(8,128)S(1)}) custom-call(bf16[64,2048]{1,0:T(8,128)(2,1)S(1)} %copy-done.2, bf16[512,2048]{1,0:T(8,128)(2,1)S(1)} %copy-done, bf16[80,256]{1,0:T(8,128)(2,1)S(1)} %collective-permute-done.6.note_b, bf16[80,256]{1,0:T(8,128)(2,1)S(1)} %collective-permute-done.7.note_a), custom_call_target="tpu_custom_call" | custom-call | tf_op jit(solution)/shard_map/push/pallas_call | solution.py:256
  26.5 3.2 %collective-permute-start.8 = (f32[512,128]{1,0:T(8,128)S(1)}, f32[512,128]{1,0:T(8,128)S(1)}, u32[]{:S(2)}, u32[]{:S(2)}) collective-permute-start(f32[512,128]{1,0:T(8,128)S(1)} %get-tuple-element.26), channel_id=1, source_target_pairs={{0,16},{16,32},{32,48},{48,64},{64,80},{80,96},{96,112},{112,128},... | collective-permute-start | bytes 786440 | tf_op jit(solution)/shard_map/ppermute | solution.py:516
  29.7 0.0 collective-permute-done.2.o1
  29.7 5.2 %collective-permute-start = (bf16[288,2048]{1,0:T(8,128)(2,1)S(1)}, bf16[288,2048]{1,0:T(8,128)(2,1)S(1)}, u32[]{:S(2)}, u32[]{:S(2)}) collective-permute-start(bf16[288,2048]{1,0:T(8,128)(2,1)S(1)} %pad_maximum_fusion), channel_id=1, source_target_pairs={{0,16},{16,32},{32,48},{48,64},{64,80},{80,96},{96,112},{112,128},... | collective-permute-start | bytes 3538952 | tf_op jit(solution)/shard_map/ppermute | solution.py:516
  34.9 0.0 collective-permute-done.3.o2
  34.9 1.9 %collective-permute-start.1 = (bf16[288,2048]{1,0:T(8,128)(2,1)S(1)}, bf16[288,2048]{1,0:T(8,128)(2,1)S(1)}, u32[]{:S(2)}, u32[]{:S(2)}) collective-permute-start(bf16[288,2048]{1,0:T(8,128)(2,1)S(1)} %pad_maximum_fusion), channel_id=1, source_target_pairs={{16,0},{32,16},{48,32},{64,48},{80,64},{96,80},{112,96},{128,112},... | collective-permute-start | bytes 3538952 | tf_op jit(solution)/shard_map/ppermute | solution.py:516
  36.8 0.1 slice.7
  37.0 0.0 collective-permute-done.4.o3
  37.0 3.9 %collective-permute-start.10 = (bf16[288,2048]{1,0:T(8,128)(2,1)S(1)}, bf16[288,2048]{1,0:T(8,128)(2,1)S(1)}, u32[]{:S(2)}, u32[]{:S(2)}) collective-permute-start(bf16[288,2048]{1,0:T(8,128)(2,1)S(1)} %slice.7), channel_id=1, source_target_pairs={{0,16},{16,32},{32,48},{48,64},{64,80},{80,96},{96,112},{112,128},... | collective-permute-start | bytes 3538952 | tf_op jit(solution)/shard_map/ppermute | solution.py:516
  40.9 0.0 collective-permute-done.5.o4
  40.9 1.9 %collective-permute-start.11 = (bf16[288,2048]{1,0:T(8,128)(2,1)S(1)}, bf16[288,2048]{1,0:T(8,128)(2,1)S(1)}, u32[]{:S(2)}, u32[]{:S(2)}) collective-permute-start(bf16[288,2048]{1,0:T(8,128)(2,1)S(1)} %slice.7), channel_id=1, source_target_pairs={{16,0},{32,16},{48,32},{64,48},{80,64},{96,80},{112,96},{128,112},... | collective-permute-start | bytes 3538952 | tf_op jit(solution)/shard_map/ppermute | solution.py:516
  42.8 5.8 %collective-permute-start.9 = (f32[512,128]{1,0:T(8,128)S(1)}, f32[512,128]{1,0:T(8,128)S(1)}, u32[]{:S(2)}, u32[]{:S(2)}) collective-permute-start(f32[512,128]{1,0:T(8,128)S(1)} %get-tuple-element.27), channel_id=1, source_target_pairs={{16,0},{32,16},{48,32},{64,48},{80,64},{96,80},{112,96},{128,112},... | collective-permute-start | bytes 786440 | tf_op jit(solution)/shard_map/ppermute | solution.py:516
  48.7 44.8 %collective-permute-done.9.from_a = f32[512,128]{1,0:T(8,128)S(1)} collective-permute-done((f32[512,128]{1,0:T(8,128)S(1)}, f32[512,128]{1,0:T(8,128)S(1)}, u32[]{:S(2)}, u32[]{:S(2)}) %collective-permute-start.9) | collective-permute-done | bytes 262176 | tf_op jit(solution)/shard_map/ppermute | solution.py:516
  93.5 6.6 %inverses.1 = (f32[512,128]{1,0:T(8,128)S(1)}, bf16[256,256]{1,0:T(8,128)(2,1)S(1)}, bf16[256,256]{1,0:T(8,128)(2,1)S(1)}, bf16[4,256,128]{2,1,0:T(8,128)(2,1)S(1)}, bf16[4,256,128]{2,1,0:T(8,128)(2,1)S(1)}) custom-call(bf16[64,2048]{1,0:T(8,128)(2,1)S(1)} %copy-done.2, bf16[512,2048]{1,0:T(8,128)(2,1)S(1)} %copy-done, bf16[512,2048]{1,0:T(8,128)(2,1)S(1)} %copy-done.3, ...), custom_call_target="tpu_custom_call" | custom-call | tf_op jit(solution)/shard_map/inverses/pallas_call | solution.py:223
  100.1 0.1 collective-permute-start.12
  100.2 1.5 %collective-permute-done.12.other = f32[512,128]{1,0:T(8,128)S(1)} collective-permute-done((f32[512,128]{1,0:T(8,128)S(1)}, f32[512,128]{1,0:T(8,128)S(1)}, u32[]{:S(2)}, u32[]{:S(2)}) %collective-permute-start.12) | collective-permute-done | bytes 262176 | tf_op jit(solution)/shard_map/ppermute | solution.py:442
  101.7 0.4 level_step.3.own.refs_4_
  102.1 0.0 copy-start.5
  102.1 2.9 %collective-permute-start.13 = (bf16[512,128]{1,0:T(8,128)(2,1)S(1)}, bf16[512,128]{1,0:T(8,128)(2,1)S(1)}, u32[]{:S(2)}, u32[]{:S(2)}) collective-permute-start(bf16[512,128]{1,0:T(8,128)(2,1)S(1)} %convert_element_type.9), channel_id=1, source_target_pairs={{0,2},{2,0},{4,6},{6,4},{8,10},{10,8},{12,14},{14,12},{16,18},{18,... | collective-permute-start | bytes 393224 | tf_op jit(solution)/shard_map/ppermute | solution.py:442
  105.0 3.9 %collective-permute-done.13.other = bf16[512,128]{1,0:T(8,128)(2,1)S(1)} collective-permute-done((bf16[512,128]{1,0:T(8,128)(2,1)S(1)}, bf16[512,128]{1,0:T(8,128)(2,1)S(1)}, u32[]{:S(2)}, u32[]{:S(2)}) %collective-permute-start.13) | collective-permute-done | bytes 131104 | tf_op jit(solution)/shard_map/ppermute | solution.py:442
  109.0 0.3 level_step.4.own.refs_5_
  109.3 3.4 %collective-permute-start.14 = (bf16[512,128]{1,0:T(8,128)(2,1)S(1)}, bf16[512,128]{1,0:T(8,128)(2,1)S(1)}, u32[]{:S(2)}, u32[]{:S(2)}) collective-permute-start(bf16[512,128]{1,0:T(8,128)(2,1)S(1)} %convert_element_type.10), channel_id=1, source_target_pairs={{0,4},{4,0},{8,12},{12,8},{16,20},{20,16},{24,28},{28,24},{32,36},... | collective-permute-start | bytes 393224 | tf_op jit(solution)/shard_map/ppermute | solution.py:442
  112.7 4.4 %collective-permute-done.14.other = bf16[512,128]{1,0:T(8,128)(2,1)S(1)} collective-permute-done((bf16[512,128]{1,0:T(8,128)(2,1)S(1)}, bf16[512,128]{1,0:T(8,128)(2,1)S(1)}, u32[]{:S(2)}, u32[]{:S(2)}) %collective-permute-start.14) | collective-permute-done | bytes 131104 | tf_op jit(solution)/shard_map/ppermute | solution.py:442
  117.1 0.3 level_step.5.refs_6_.v3
  117.4 3.6 %collective-permute-start.15 = (bf16[512,128]{1,0:T(8,128)(2,1)S(1)}, bf16[512,128]{1,0:T(8,128)(2,1)S(1)}, u32[]{:S(2)}, u32[]{:S(2)}) collective-permute-start(bf16[512,128]{1,0:T(8,128)(2,1)S(1)} %convert_element_type.11), channel_id=1, source_target_pairs={{0,8},{8,0},{16,24},{24,16},{32,40},{40,32},{48,56},{56,48},{64,72... | collective-permute-start | bytes 393224 | tf_op jit(solution)/shard_map/ppermute | solution.py:442
  121.0 6.8 %own_near.1.base = f32[512,2048]{1,0:T(8,128)S(1)} custom-call(s32[4,4]{1,0:T(4,128)S(1)} %copy-done.5, bf16[64,2048]{1,0:T(8,128)(2,1)S(1)} %copy-done.2, bf16[512,2048]{1,0:T(8,128)(2,1)S(1)} %copy-done, bf16[512,2048]{1,0:T(8,128)(2,1)S(1)} %copy-done.3), custom_call_target="tpu_custom_call" | custom-call | tf_op jit(solution)/shard_map/own_near/pallas_call | solution.py:302
  127.8 0.6 tables.1
  128.4 0.0 collective-permute-done.before
  128.4 2.9 %near_tiles.1.tiles = bf16[16,512,512]{2,1,0:T(8,128)(2,1)S(1)} custom-call(s32[4,4]{1,0:T(4,128)S(1)} %copy-done.5, bf16[64,2048]{1,0:T(8,128)(2,1)S(1)} %copy-done.2, bf16[288,2048]{1,0:T(8,128)(2,1)S(1)} %collective-permute-done.before, bf16[288,2048]{1,0:T(8,128)(2,1)S(1)} %collective-permute-done.1.after), custom_call_target="tpu_custom_call" | custom-call | tf_op jit(solution)/shard_map/near_tiles/pallas_call | solution.py:362
  131.4 3.6 %near_part.2 = (f32[224,2048]{1,0:T(8,128)S(1)}, f32[224,256]{1,0:T(8,128)S(1)}) custom-call(s32[4,4]{1,0:T(4,128)S(1)} %copy-done.5, f32[512,2048]{1,0:T(8,128)S(1)} %own_near.1.base, bf16[288,2048]{1,0:T(8,128)(2,1)S(1)} %collective-permute-done.before, bf16[288,2048]{1,0:T(8,128)(2,1)S(1)} %collective-permute-done.1.after, ...), custom_call_target="tpu_custom_call" | custom-call | tf_op jit(solution)/shard_map/near_part/pallas_call | solution.py:401
  135.0 0.0 collective-permute-done.10.before
  135.0 0.0 collective-permute-done.11.after
  135.0 4.0 %near_part.3 = (f32[288,2048]{1,0:T(8,128)S(1)}, f32[288,256]{1,0:T(8,128)S(1)}) custom-call(s32[4,4]{1,0:T(4,128)S(1)} %copy-done.5, f32[512,2048]{1,0:T(8,128)S(1)} %own_near.1.base, bf16[288,2048]{1,0:T(8,128)(2,1)S(1)} %collective-permute-done.10.before, bf16[288,2048]{1,0:T(8,128)(2,1)S(1)} %collective-permute-done.11.after, ...), custom_call_target="tpu_custom_call" | custom-call | tf_op jit(solution)/shard_map/near_part/pallas_call | solution.py:401
  139.0 1.9 %settle.1 = (f32[512,2048]{1,0:T(8,128)S(1)}, f32[512,256]{1,0:T(8,128)S(1)}) custom-call(s32[4,4]{1,0:T(4,128)S(1)} %copy-done.5, f32[224,2048]{1,0:T(8,128)S(1)} %get-tuple-element.30.refs_0_, f32[224,256]{1,0:T(8,128)S(1)} %get-tuple-element.31.refs_1_, f32[288,2048]{1,0:T(8,128)S(1)} %get-tuple-element.32.refs_2_, ...), custom_call_target="tpu_custom_call" | custom-call | tf_op jit(solution)/shard_map/settle/pallas_call | solution.py:466
  140.9 0.0 collective-permute-done.15.w4
  140.9 3.8 %finish.1 = f32[512,2048]{1,0:T(8,128)} custom-call(s32[4,4]{1,0:T(4,128)S(1)} %copy-done.5, f32[512,2048]{1,0:T(8,128)S(1)} %get-tuple-element.38.ready, f32[512,256]{1,0:T(8,128)S(1)} %get-tuple-element.39.corr, f32[512,128]{1,0:T(8,128)S(1)} %level_step.5.refs_6_.v3, bf16[512,128]{1,0:T(8,128)(2,1)S(1)} %collective-permute-done.15.w4, ...), custom_call_target="tpu_custom_call" | custom-call | tf_op jit(solution)/shard_map/finish/pallas_call | solution.py:502
  (18 shorter events, 0.1 us)
Async XLA Ops:
  0.0 18.2 %copy-start.2 = (bf16[64,2048]{1,0:T(8,128)(2,1)S(1)}, bf16[64,2048]{1,0:T(8,128)(2,1)}, u32[]{:S(2)}) copy-start(bf16[64,2048]{1,0:T(8,128)(2,1)} %pts.9) | copy-start | bytes 786436
  0.0 18.2 %slice-start = ((bf16[512,2048]{1,0:T(8,128)(2,1)}), bf16[224,2048]{1,0:T(8,128)(2,1)S(1)}, s32[]{:S(2)}) async-start(bf16[512,2048]{1,0:T(8,128)(2,1)} %w.5), calls=%async_computation | async-start | bytes 1835008 | tf_op jit(solution)/shard_map/slice | solution.py:532
  2.4 13.4 %collective-permute-start.6 = (bf16[80,256]{1,0:T(8,128)(2,1)}, bf16[80,256]{1,0:T(8,128)(2,1)S(1)}, u32[]{:S(2)}, u32[]{:S(2)}) collective-permute-start(bf16[80,256]{1,0:T(8,128)(2,1)} %get-tuple-element.24.note), channel_id=1, source_target_pairs={{0,16},{16,32},{32,48},{48,64},{64,80},{80,96},{96,112},{112,128},... | collective-permute-start | bytes 122888 | tf_op jit(solution)/shard_map/ppermute | solution.py:516
  5.9 16.0 %copy-start = (bf16[512,2048]{1,0:T(8,128)(2,1)S(1)}, bf16[512,2048]{1,0:T(8,128)(2,1)}, u32[]{:S(2)}) copy-start(bf16[512,2048]{1,0:T(8,128)(2,1)} %w.5) | copy-start | bytes 6291460
  5.9 23.8 %collective-permute-start.2 = (bf16[64,128]{1,0:T(8,128)(2,1)}, bf16[64,128]{1,0:T(8,128)(2,1)S(1)}, u32[]{:S(2)}, u32[]{:S(2)}) collective-permute-start(bf16[64,128]{1,0:T(8,128)(2,1)} %get-tuple-element.25.kept), channel_id=1, source_target_pairs={{0,1},{1,0},{2,3},{3,2},{4,5},{5,4},{6,7},{7,6},{8,9},{9,8},{10,11... | collective-permute-start | bytes 49160 | tf_op jit(solution)/shard_map/ppermute | solution.py:442
  6.0 28.9 %collective-permute-start.3 = (bf16[64,128]{1,0:T(8,128)(2,1)}, bf16[64,128]{1,0:T(8,128)(2,1)S(1)}, u32[]{:S(2)}, u32[]{:S(2)}) collective-permute-start(bf16[64,128]{1,0:T(8,128)(2,1)} %get-tuple-element.25.kept), channel_id=1, source_target_pairs={{0,2},{1,3},{2,0},{3,1},{4,6},{5,7},{6,4},{7,5},{8,10},{9,11},{10,... | collective-permute-start | bytes 49160 | tf_op jit(solution)/shard_map/ppermute | solution.py:442
  8.0 28.9 %collective-permute-start.4 = (bf16[64,128]{1,0:T(8,128)(2,1)}, bf16[64,128]{1,0:T(8,128)(2,1)S(1)}, u32[]{:S(2)}, u32[]{:S(2)}) collective-permute-start(bf16[64,128]{1,0:T(8,128)(2,1)} %get-tuple-element.25.kept), channel_id=1, source_target_pairs={{0,4},{1,5},{2,6},{3,7},{4,0},{5,1},{6,2},{7,3},{8,12},{9,13},{10,... | collective-permute-start | bytes 49160 | tf_op jit(solution)/shard_map/ppermute | solution.py:442
  11.3 29.6 %collective-permute-start.5 = (bf16[64,128]{1,0:T(8,128)(2,1)}, bf16[64,128]{1,0:T(8,128)(2,1)S(1)}, u32[]{:S(2)}, u32[]{:S(2)}) collective-permute-start(bf16[64,128]{1,0:T(8,128)(2,1)} %get-tuple-element.25.kept), channel_id=1, source_target_pairs={{0,8},{1,9},{2,10},{3,11},{4,12},{5,13},{6,14},{7,15},{8,0},{9,1},... | collective-permute-start | bytes 49160 | tf_op jit(solution)/shard_map/ppermute | solution.py:442
  15.8 6.1 %collective-permute-start.7 = (bf16[80,256]{1,0:T(8,128)(2,1)}, bf16[80,256]{1,0:T(8,128)(2,1)S(1)}, u32[]{:S(2)}, u32[]{:S(2)}) collective-permute-start(bf16[80,256]{1,0:T(8,128)(2,1)} %get-tuple-element.24.note), channel_id=1, source_target_pairs={{16,0},{32,16},{48,32},{64,48},{80,64},{96,80},{112,96},{128,112},... | collective-permute-start | bytes 122888 | tf_op jit(solution)/shard_map/ppermute | solution.py:516
  18.3 75.1 %copy-start.1 = (bf16[2048,256]{1,0:T(8,128)(2,1)S(1)}, bf16[2048,256]{1,0:T(8,128)(2,1)}, u32[]{:S(2)}) copy-start(bf16[2048,256]{1,0:T(8,128)(2,1)} %get-tuple-element.23.pick) | copy-start | bytes 3145732
  18.3 75.1 %copy-start.3 = (bf16[512,2048]{1,0:T(8,128)(2,1)S(1)}, bf16[512,2048]{1,0:T(8,128)(2,1)}, u32[]{:S(2)}) copy-start(bf16[512,2048]{1,0:T(8,128)(2,1)} %targets.3) | copy-start | bytes 6291460
  18.3 75.1 %copy-start.4 = (bf16[80,256]{1,0:T(8,128)(2,1)S(1)}, bf16[80,256]{1,0:T(8,128)(2,1)}, u32[]{:S(2)}) copy-start(bf16[80,256]{1,0:T(8,128)(2,1)} %get-tuple-element.24.note) | copy-start | bytes 122884
  18.3 75.1 %copy-start.6 = (bf16[64,128]{1,0:T(8,128)(2,1)S(1)}, bf16[64,128]{1,0:T(8,128)(2,1)}, u32[]{:S(2)}) copy-start(bf16[64,128]{1,0:T(8,128)(2,1)} %get-tuple-element.25.kept) | copy-start | bytes 49156
  26.5 16.3 %collective-permute-start.8 = (f32[512,128]{1,0:T(8,128)S(1)}, f32[512,128]{1,0:T(8,128)S(1)}, u32[]{:S(2)}, u32[]{:S(2)}) collective-permute-start(f32[512,128]{1,0:T(8,128)S(1)} %get-tuple-element.26), channel_id=1, source_target_pairs={{0,16},{16,32},{32,48},{48,64},{64,80},{80,96},{96,112},{112,128},... | collective-permute-start | bytes 786440 | tf_op jit(solution)/shard_map/ppermute | solution.py:516
  29.7 98.7 %collective-permute-start = (bf16[288,2048]{1,0:T(8,128)(2,1)S(1)}, bf16[288,2048]{1,0:T(8,128)(2,1)S(1)}, u32[]{:S(2)}, u32[]{:S(2)}) collective-permute-start(bf16[288,2048]{1,0:T(8,128)(2,1)S(1)} %pad_maximum_fusion), channel_id=1, source_target_pairs={{0,16},{16,32},{32,48},{48,64},{64,80},{80,96},{96,112},{112,128},... | collective-permute-start | bytes 3538952 | tf_op jit(solution)/shard_map/ppermute | solution.py:516
  34.9 93.5 %collective-permute-start.1 = (bf16[288,2048]{1,0:T(8,128)(2,1)S(1)}, bf16[288,2048]{1,0:T(8,128)(2,1)S(1)}, u32[]{:S(2)}, u32[]{:S(2)}) collective-permute-start(bf16[288,2048]{1,0:T(8,128)(2,1)S(1)} %pad_maximum_fusion), channel_id=1, source_target_pairs={{16,0},{32,16},{48,32},{64,48},{80,64},{96,80},{112,96},{128,112},... | collective-permute-start | bytes 3538952 | tf_op jit(solution)/shard_map/ppermute | solution.py:516
  37.0 98.0 %collective-permute-start.10 = (bf16[288,2048]{1,0:T(8,128)(2,1)S(1)}, bf16[288,2048]{1,0:T(8,128)(2,1)S(1)}, u32[]{:S(2)}, u32[]{:S(2)}) collective-permute-start(bf16[288,2048]{1,0:T(8,128)(2,1)S(1)} %slice.7), channel_id=1, source_target_pairs={{0,16},{16,32},{32,48},{48,64},{64,80},{80,96},{96,112},{112,128},... | collective-permute-start | bytes 3538952 | tf_op jit(solution)/shard_map/ppermute | solution.py:516
  40.9 94.1 %collective-permute-start.11 = (bf16[288,2048]{1,0:T(8,128)(2,1)S(1)}, bf16[288,2048]{1,0:T(8,128)(2,1)S(1)}, u32[]{:S(2)}, u32[]{:S(2)}) collective-permute-start(bf16[288,2048]{1,0:T(8,128)(2,1)S(1)} %slice.7), channel_id=1, source_target_pairs={{16,0},{32,16},{48,32},{64,48},{80,64},{96,80},{112,96},{128,112},... | collective-permute-start | bytes 3538952 | tf_op jit(solution)/shard_map/ppermute | solution.py:516
  42.8 50.6 %collective-permute-start.9 = (f32[512,128]{1,0:T(8,128)S(1)}, f32[512,128]{1,0:T(8,128)S(1)}, u32[]{:S(2)}, u32[]{:S(2)}) collective-permute-start(f32[512,128]{1,0:T(8,128)S(1)} %get-tuple-element.27), channel_id=1, source_target_pairs={{16,0},{32,16},{48,32},{64,48},{80,64},{96,80},{112,96},{128,112},... | collective-permute-start | bytes 786440 | tf_op jit(solution)/shard_map/ppermute | solution.py:516
  100.1 1.6 %collective-permute-start.12 = (f32[512,128]{1,0:T(8,128)S(1)}, f32[512,128]{1,0:T(8,128)S(1)}, u32[]{:S(2)}, u32[]{:S(2)}) collective-permute-start(f32[512,128]{1,0:T(8,128)S(1)} %get-tuple-element.34.own), channel_id=1, source_target_pairs={{0,1},{1,0},{2,3},{3,2},{4,5},{5,4},{6,7},{7,6},{8,9},{9,8},{10,11... | collective-permute-start | bytes 786440 | tf_op jit(solution)/shard_map/ppermute | solution.py:442
  102.1 18.9 %copy-start.5 = (s32[4,4]{1,0:T(4,128)S(1)}, s32[4,4]{1,0:T(4,128)}, u32[]{:S(2)}) copy-start(s32[4,4]{1,0:T(4,128)} %lists.11) | copy-start | bytes 196
  102.1 6.9 %collective-permute-start.13 = (bf16[512,128]{1,0:T(8,128)(2,1)S(1)}, bf16[512,128]{1,0:T(8,128)(2,1)S(1)}, u32[]{:S(2)}, u32[]{:S(2)}) collective-permute-start(bf16[512,128]{1,0:T(8,128)(2,1)S(1)} %convert_element_type.9), channel_id=1, source_target_pairs={{0,2},{2,0},{4,6},{6,4},{8,10},{10,8},{12,14},{14,12},{16,18},{18,... | collective-permute-start | bytes 393224 | tf_op jit(solution)/shard_map/ppermute | solution.py:442
  109.3 7.8 %collective-permute-start.14 = (bf16[512,128]{1,0:T(8,128)(2,1)S(1)}, bf16[512,128]{1,0:T(8,128)(2,1)S(1)}, u32[]{:S(2)}, u32[]{:S(2)}) collective-permute-start(bf16[512,128]{1,0:T(8,128)(2,1)S(1)} %convert_element_type.10), channel_id=1, source_target_pairs={{0,4},{4,0},{8,12},{12,8},{16,20},{20,16},{24,28},{28,24},{32,36},... | collective-permute-start | bytes 393224 | tf_op jit(solution)/shard_map/ppermute | solution.py:442
  117.4 23.5 %collective-permute-start.15 = (bf16[512,128]{1,0:T(8,128)(2,1)S(1)}, bf16[512,128]{1,0:T(8,128)(2,1)S(1)}, u32[]{:S(2)}, u32[]{:S(2)}) collective-permute-start(bf16[512,128]{1,0:T(8,128)(2,1)S(1)} %convert_element_type.11), channel_id=1, source_target_pairs={{0,8},{8,0},{16,24},{24,16},{32,40},{40,32},{48,56},{56,48},{64,72... | collective-permute-start | bytes 393224 | tf_op jit(solution)/shard_map/ppermute | solution.py:442

commit v2 on v1

--- a/solution.py
+++ b/solution.py
@@ -12,7 +12,7 @@
 N_LEAF = 16
 RIDGE = 0.5
 SHIFT = 4.0
-EARLY_ROWS = 224
+EARLY_ROWS = 192
 COARSE_STEPS = 4
 FINE_STEPS = 2
 
@@ -47,14 +47,13 @@
         out = jnp.where(row == at + 1, mid, out)
         return jnp.where(row == at + 2, low, out).astype(bf16)
 
-    left = jnp.concatenate([x, tail(0, 3)], axis=0)
+    left = jnp.concatenate([x, tail(0, 3)], axis=0).T
     right = jnp.concatenate([x, tail(3, 0)], axis=0)
     return left, right
 
 
 def kernel_of(left, right, features):
-    half = lax.dot_general(left, right, (((0,), (0,)), ((), ())), preferred_element_type=f32)
-    return jnp.exp((4.0 / features) * half)
+    return jnp.exp((4.0 / features) * mm(left, right))
 
 
 def leaf_of(lists):
@@ -114,7 +113,7 @@
             pltpu.VMEM(skeleton.shape, jnp.int32),
             pltpu.SemaphoreType.DMA((3,)),
         ],
-        compiler_params=params(60),
+        compiler_params=params(),
         name="prep",
     )(near_lists, points, skeleton)
 
@@ -174,7 +173,7 @@
     features = ref.shape[0] - 16
     cols = slice(j * CLUSTER_PTS, (j + 1) * CLUSTER_PTS)
     flags = ref[features + begin + j : features + begin + j + 1, :].astype(f32)
-    tile = kernel_of(left[:, cols], right, features) * flags
+    tile = kernel_of(left[cols, :], right, features) * flags
     term = mm(w[:, cols], tile.astype(bf16))
     if j == 0:
         total[...] = term
@@ -187,7 +186,7 @@
     return mm(vh, high) + (mm(vh, low) + mm(vl, high))
 
 
-def inverse_kernel(pts, w, targets, pick, note, kept, o1, o2, o3, o4, from_b, from_a, start, a_high, a_low, b_high, b_low, left, total):
+def inverse_kernel(pts, w, targets, pick, note, kept, o1, o2, o3, o4, mine, a_high, a_low, b_high, b_low, left, total):
     features, half = kept.shape
     clusters = pts.shape[1] // CLUSTER_PTS
     left[...] = lifted(pts[...])[0]
@@ -210,10 +209,10 @@
     a_high[...], a_low[...] = ah, al
     for k in range(4):
         b_high[k], b_low[k] = split(SHIFT * found[k + 1])
-    start[...] = solve_rows(total[...], ah[:, :half], al[:, :half]) - from_b[...] - from_a[...]
-
-
-def inverses(points, weights, targets, pick, note, kept, others, from_b, from_a):
+    mine[...] = solve_rows(total[...], ah[:, :half], al[:, :half])
+
+
+def inverses(points, weights, targets, pick, note, kept, others):
     features, n = points.shape
     rows = weights.shape[0]
     half = kept.shape[1]
@@ -223,12 +222,12 @@
     return pl.pallas_call(
         inverse_kernel,
         out_shape=(jax.ShapeDtypeStruct((rows, half), f32), full, full, part, part),
-        in_specs=[VMEM] * 12,
+        in_specs=[VMEM] * 10,
         out_specs=(VMEM,) * 5,
-        scratch_shapes=[pltpu.VMEM((features + 16, n), bf16), pltpu.VMEM((rows, s), f32)],
+        scratch_shapes=[pltpu.VMEM((n, features + 16), bf16), pltpu.VMEM((rows, s), f32)],
         compiler_params=params(),
         name="inverses",
-    )(points, weights, targets, pick, note, kept, *others, from_b, from_a)
+    )(points, weights, targets, pick, note, kept, *others)
 
 
 def push_kernel(pts, w, note_b, note_a, to_b, to_a, left, total):
@@ -258,10 +257,25 @@
         out_shape=(jax.ShapeDtypeStruct((rows, s // 2), f32),) * 2,
         in_specs=[VMEM] * 4,
         out_specs=(VMEM,) * 2,
-        scratch_shapes=[pltpu.VMEM((features + 16, n), bf16), pltpu.VMEM((2, rows, s), f32)],
+        scratch_shapes=[pltpu.VMEM((n, features + 16), bf16), pltpu.VMEM((2, rows, s), f32)],
         compiler_params=params(),
         name="push",
     )(points, weights, note_b, note_a)
+
+
+def join_kernel(mine, from_b, from_a, out):
+    out[...] = mine[...] - from_b[...] - from_a[...]
+
+
+def join(mine, from_b, from_a):
+    return pl.pallas_call(
+        join_kernel,
+        out_shape=jax.ShapeDtypeStruct(mine.shape, f32),
+        in_specs=[VMEM] * 3,
+        out_specs=VMEM,
+        compiler_params=params(),
+        name="join",
+    )(mine, from_b, from_a)
 
 
 def is_live(lists, g, slot):
@@ -282,19 +296,28 @@
 def own_kernel(lists, pts, w, targets, out, left, right, tile):
     features = pts.shape[0]
     left[...], right[...] = lifted(pts[...])
-    out[...] = targets[...].astype(f32) - RIDGE * w[...].astype(f32)
+    slots = lists.shape[1]
 
     def step(i, carry):
         live, way, cols, own = pair_of(lists, i)
 
         @pl.when(live & (way == 0))
         def _():
-            tile[...] = kernel_of(left[:, cols], right[:, own], features).astype(bf16)
-            out[:, own] -= mm(w[:, cols], tile[...])
+            tile[...] = kernel_of(left[cols, :], right[:, own], features).astype(bf16)
+            term = mm(w[:, cols], tile[...])
+
+            @pl.when(i % slots == 0)
+            def _():
+                plain = targets[:, own].astype(f32) - RIDGE * w[:, own].astype(f32)
+                out[:, own] = plain - term
+
+            @pl.when(i % slots != 0)
+            def _():
+                out[:, own] -= term
 
         return carry
 
-    lax.fori_loop(0, lists.shape[0] * lists.shape[1], step, 0)
+    lax.fori_loop(0, lists.shape[0] * slots, step, 0)
 
 
 def own_near(points, weights, targets, near_lists):
@@ -305,7 +328,7 @@
         in_specs=[SMEM] + [VMEM] * 3,
         out_specs=VMEM,
         scratch_shapes=[
-            pltpu.VMEM((features + 16, n), bf16),
+            pltpu.VMEM((n, features + 16), bf16),
             pltpu.VMEM((features + 16, n), bf16),
             pltpu.VMEM((CLUSTER_PTS, CLUSTER_PTS), bf16),
         ],
@@ -344,11 +367,11 @@
 
         @pl.when(live & (way < 0))
         def _():
-            out[i] = kernel_of(lb[:, cols], right[:, own], features).astype(bf16)
+            out[i] = kernel_of(lb[cols, :], right[:, own], features).astype(bf16)
 
         @pl.when(live & (way > 0))
         def _():
-            out[i] = kernel_of(la[:, cols], right[:, own], features).astype(bf16)
+            out[i] = kernel_of(la[cols, :], right[:, own], features).astype(bf16)
 
         return carry
 
@@ -365,7 +388,8 @@
         grid=(1,),
         in_specs=[SMEM, VMEM, head, head],
         out_specs=VMEM,
-        scratch_shapes=[pltpu.VMEM((features + 16, n), bf16)] * 3,
+        scratch_shapes=[pltpu.VMEM((n, features + 16), bf16)] * 2
+        + [pltpu.VMEM((features + 16, n), bf16)],
         compiler_params=params(),
         name="near_tiles",
     )(near_lists, points, before, after)
@@ -538,10 +562,11 @@
     before_2, after_2 = both_ways(second)
     swaps = [[(i, i ^ (1 << k)) for i in range(size)] for k in range(4)]
     others = [among_leaves(kept, swaps[k]) for k in range(4)]
-    v0, a_high, a_low, b_high, b_low = inverses(
-        points, weights, targets, pick, note, kept, others, from_b, from_a
+    mine, a_high, a_low, b_high, b_low = inverses(
+        points, weights, targets, pick, note, kept, others
     )
 
+    v0 = join(mine, from_b, from_a)
     base = own_near(points, weights, targets, near_lists)
     tiles = near_tiles(points, before_1, after_1, near_lists)
     shared = (tiles, pick, a_high, a_low, near_lists)

time: 145 us -> 130 us (0.90)
  the two profiles are of different devices: /device:TPU:10 before, /device:TPU:24 now
where the time goes in v2:
time: 130 us
  starting transfers between devices  52.7 us (41%)
  waiting for transfers between devices  36.5 us (28%)
  Pallas kernels  36.2 us (28%)
  local copies, waits for them, and re-layouts  3.78 us (3%)
    ppermute x8, waiting for transfers between devices, shifted(): return lax.ppermute(value, 'clus', pairs)  27.4 us
    ppermute x8, starting transfers between devices, shifted(): return lax.ppermute(value, 'clus', pairs)  27 us
    ppermute x8, starting transfers between devices, among_leaves(): return lax.ppermute(value, 'leaf', pairs)  25.7 us
    ppermute x8, waiting for transfers between devices, among_leaves(): return lax.ppermute(value, 'leaf', pairs)  9.14 us
    pallas_call x2, Pallas kernels, near_part(): pl.pallas_call(functools.partial(near_kernel, first, skip), out_shape=(ja...  7.53 us
    pallas_call x1, Pallas kernels, inverses(): pl.pallas_call(inverse_kernel, out_shape=(jax.ShapeDtypeStruct((rows, hal...  6.6 us
    pallas_call x1, Pallas kernels, own_near(): pl.pallas_call(own_kernel, out_shape=jax.ShapeDtypeStruct(weights.shape,...  5.99 us
    pallas_call x1, Pallas kernels, push(): pl.pallas_call(push_kernel, out_shape=(jax.ShapeDtypeStruct((rows, s // 2...  4.6 us
  transfers between devices with their start and end apart: 16, of which 5 were waited for; matrix products, arithmetic and copies ran while one was open for 1% of the time, Pallas kernels for 24%

profile of v2, /device:TPU:24, one launch (start us, length us, event | category | flops | bytes accessed | tf_op | source)
XLA Modules:
  0.0 129.9 jit_solution(5298826952267807308)
XLA Ops:
  0.0 0.9 copy-done.1
  1.0 0.7 copy-done.4
  1.6 0.7 copy-done.5
  2.3 1.1 prep.1
  3.5 3.1 %collective-permute-start.8 = (bf16[80,256]{1,0:T(8,128)(2,1)S(1)}, bf16[80,256]{1,0:T(8,128)(2,1)S(1)}, u32[]{:S(2)}, u32[]{:S(2)}) collective-permute-start(bf16[80,256]{1,0:T(8,128)(2,1)S(1)} %get-tuple-element.24.note), channel_id=1, source_target_pairs={{0,16},{16,32},{32,48},{48,64},{64,80},{80,96},{96,112},{112,128},... | collective-permute-start | bytes 122888 | tf_op jit(solution)/shard_map/ppermute | solution.py:540
  6.5 2.8 %collective-permute-start.9 = (bf16[80,256]{1,0:T(8,128)(2,1)S(1)}, bf16[80,256]{1,0:T(8,128)(2,1)S(1)}, u32[]{:S(2)}, u32[]{:S(2)}) collective-permute-start(bf16[80,256]{1,0:T(8,128)(2,1)S(1)} %get-tuple-element.24.note), channel_id=1, source_target_pairs={{16,0},{32,16},{48,32},{64,48},{80,64},{96,80},{112,96},{128,112},... | collective-permute-start | bytes 122888 | tf_op jit(solution)/shard_map/ppermute | solution.py:540
  9.3 0.0 copy-start
  9.3 0.1 collective-permute-start.2
  9.4 2.0 %collective-permute-start.3 = (bf16[64,128]{1,0:T(8,128)(2,1)S(1)}, bf16[64,128]{1,0:T(8,128)(2,1)S(1)}, u32[]{:S(2)}, u32[]{:S(2)}) collective-permute-start(bf16[64,128]{1,0:T(8,128)(2,1)S(1)} %get-tuple-element.25.kept), channel_id=1, source_target_pairs={{0,2},{1,3},{2,0},{3,1},{4,6},{5,7},{6,4},{7,5},{8,10},{9,11},{10,... | collective-permute-start | bytes 49160 | tf_op jit(solution)/shard_map/ppermute | solution.py:466
  11.4 1.4 %slice.7 = bf16[320,2048]{1,0:T(8,128)(2,1)S(1)} slice(bf16[512,2048]{1,0:T(8,128)(2,1)} %w.5), slice={[192:512], [0:2048]} | slice | bytes 2621440 | tf_op jit(solution)/shard_map/slice | solution.py:561
  12.9 0.0 slice-start
  12.9 5.3 %collective-permute-start.6 = (bf16[320,2048]{1,0:T(8,128)(2,1)S(1)}, bf16[320,2048]{1,0:T(8,128)(2,1)S(1)}, u32[]{:S(2)}, u32[]{:S(2)}) collective-permute-start(bf16[320,2048]{1,0:T(8,128)(2,1)S(1)} %slice.7), channel_id=1, source_target_pairs={{0,16},{16,32},{32,48},{48,64},{64,80},{80,96},{96,112},{112,128},... | collective-permute-start | bytes 3932168 | tf_op jit(solution)/shard_map/ppermute | solution.py:540
  18.2 0.0 collective-permute-done.8.note_b
  18.2 1.9 %collective-permute-start.7 = (bf16[320,2048]{1,0:T(8,128)(2,1)S(1)}, bf16[320,2048]{1,0:T(8,128)(2,1)S(1)}, u32[]{:S(2)}, u32[]{:S(2)}) collective-permute-start(bf16[320,2048]{1,0:T(8,128)(2,1)S(1)} %slice.7), channel_id=1, source_target_pairs={{16,0},{32,16},{48,32},{64,48},{80,64},{96,80},{112,96},{128,112},... | collective-permute-start | bytes 3932168 | tf_op jit(solution)/shard_map/ppermute | solution.py:540
  20.1 0.0 copy-start.3
  20.2 0.0 collective-permute-done.9.note_a
  20.2 3.4 %collective-permute-start.4 = (bf16[64,128]{1,0:T(8,128)(2,1)S(1)}, bf16[64,128]{1,0:T(8,128)(2,1)S(1)}, u32[]{:S(2)}, u32[]{:S(2)}) collective-permute-start(bf16[64,128]{1,0:T(8,128)(2,1)S(1)} %get-tuple-element.25.kept), channel_id=1, source_target_pairs={{0,4},{1,5},{2,6},{3,7},{4,0},{5,1},{6,2},{7,3},{8,12},{9,13},{10,... | collective-permute-start | bytes 49160 | tf_op jit(solution)/shard_map/ppermute | solution.py:466
  23.5 4.6 %push.1 = (f32[512,128]{1,0:T(8,128)S(1)}, f32[512,128]{1,0:T(8,128)S(1)}) custom-call(bf16[64,2048]{1,0:T(8,128)(2,1)S(1)} %copy-done.1, bf16[512,2048]{1,0:T(8,128)(2,1)S(1)} %copy-done, bf16[80,256]{1,0:T(8,128)(2,1)S(1)} %collective-permute-done.8.note_b, bf16[80,256]{1,0:T(8,128)(2,1)S(1)} %collective-permute-done.9.note_a), custom_call_target="tpu_custom_call" | custom-call | tf_op jit(solution)/shard_map/push/pallas_call | solution.py:255
  28.1 0.0 collective-permute-done.2.o1
  28.2 4.6 %collective-permute-start.5 = (bf16[64,128]{1,0:T(8,128)(2,1)S(1)}, bf16[64,128]{1,0:T(8,128)(2,1)S(1)}, u32[]{:S(2)}, u32[]{:S(2)}) collective-permute-start(bf16[64,128]{1,0:T(8,128)(2,1)S(1)} %get-tuple-element.25.kept), channel_id=1, source_target_pairs={{0,8},{1,9},{2,10},{3,11},{4,12},{5,13},{6,14},{7,15},{8,0},{9,1},... | collective-permute-start | bytes 49160 | tf_op jit(solution)/shard_map/ppermute | solution.py:466
  32.7 6.0 %collective-permute-start.10 = (f32[512,128]{1,0:T(8,128)S(1)}, f32[512,128]{1,0:T(8,128)S(1)}, u32[]{:S(2)}, u32[]{:S(2)}) collective-permute-start(f32[512,128]{1,0:T(8,128)S(1)} %get-tuple-element.33), channel_id=1, source_target_pairs={{0,16},{16,32},{32,48},{48,64},{64,80},{80,96},{96,112},{112,128},... | collective-permute-start | bytes 786440 | tf_op jit(solution)/shard_map/ppermute | solution.py:540
  38.8 0.1 pad_maximum_fusion
  38.9 0.0 collective-permute-done.4.o3
  38.9 1.9 %collective-permute-start = (bf16[256,2048]{1,0:T(8,128)(2,1)S(1)}, bf16[256,2048]{1,0:T(8,128)(2,1)S(1)}, u32[]{:S(2)}, u32[]{:S(2)}) collective-permute-start(bf16[256,2048]{1,0:T(8,128)(2,1)S(1)} %pad_maximum_fusion), channel_id=1, source_target_pairs={{0,16},{16,32},{32,48},{48,64},{64,80},{80,96},{96,112},{112,128},... | collective-permute-start | bytes 3145736 | tf_op jit(solution)/shard_map/ppermute | solution.py:540
  40.8 3.9 %collective-permute-start.1 = (bf16[256,2048]{1,0:T(8,128)(2,1)S(1)}, bf16[256,2048]{1,0:T(8,128)(2,1)S(1)}, u32[]{:S(2)}, u32[]{:S(2)}) collective-permute-start(bf16[256,2048]{1,0:T(8,128)(2,1)S(1)} %pad_maximum_fusion), channel_id=1, source_target_pairs={{16,0},{32,16},{48,32},{64,48},{80,64},{96,80},{112,96},{128,112},... | collective-permute-start | bytes 3145736 | tf_op jit(solution)/shard_map/ppermute | solution.py:540
  44.8 8.2 %collective-permute-done.10.from_b = f32[512,128]{1,0:T(8,128)S(1)} collective-permute-done((f32[512,128]{1,0:T(8,128)S(1)}, f32[512,128]{1,0:T(8,128)S(1)}, u32[]{:S(2)}, u32[]{:S(2)}) %collective-permute-start.10) | collective-permute-done | bytes 262176 | tf_op jit(solution)/shard_map/ppermute | solution.py:540
  53.0 2.1 %collective-permute-start.11 = (f32[512,128]{1,0:T(8,128)S(1)}, f32[512,128]{1,0:T(8,128)S(1)}, u32[]{:S(2)}, u32[]{:S(2)}) collective-permute-start(f32[512,128]{1,0:T(8,128)S(1)} %get-tuple-element.34), channel_id=1, source_target_pairs={{16,0},{32,16},{48,32},{64,48},{80,64},{96,80},{112,96},{128,112},... | collective-permute-start | bytes 786440 | tf_op jit(solution)/shard_map/ppermute | solution.py:540
  55.1 6.6 %inverses.1 = (f32[512,128]{1,0:T(8,128)S(1)}, bf16[256,256]{1,0:T(8,128)(2,1)S(1)}, bf16[256,256]{1,0:T(8,128)(2,1)S(1)}, bf16[4,256,128]{2,1,0:T(8,128)(2,1)S(1)}, bf16[4,256,128]{2,1,0:T(8,128)(2,1)S(1)}) custom-call(bf16[64,2048]{1,0:T(8,128)(2,1)S(1)} %copy-done.1, bf16[512,2048]{1,0:T(8,128)(2,1)S(1)} %copy-done, bf16[512,2048]{1,0:T(8,128)(2,1)S(1)} %copy-done.3, ...), custom_call_target="tpu_custom_call" | custom-call | tf_op jit(solution)/shard_map/inverses/pallas_call | solution.py:222
  61.7 19.2 %collective-permute-done.11.from_a = f32[512,128]{1,0:T(8,128)S(1)} collective-permute-done((f32[512,128]{1,0:T(8,128)S(1)}, f32[512,128]{1,0:T(8,128)S(1)}, u32[]{:S(2)}, u32[]{:S(2)}) %collective-permute-start.11) | collective-permute-done | bytes 262176 | tf_op jit(solution)/shard_map/ppermute | solution.py:540
  80.9 0.1 collective-permute-start.12
  81.0 1.5 %collective-permute-done.12.other = f32[512,128]{1,0:T(8,128)S(1)} collective-permute-done((f32[512,128]{1,0:T(8,128)S(1)}, f32[512,128]{1,0:T(8,128)S(1)}, u32[]{:S(2)}, u32[]{:S(2)}) %collective-permute-start.12) | collective-permute-done | bytes 262176 | tf_op jit(solution)/shard_map/ppermute | solution.py:466
  82.5 0.4 level_step.3.own.refs_4_
  82.9 0.0 copy-start.2
  82.9 2.3 %collective-permute-start.13 = (bf16[512,128]{1,0:T(8,128)(2,1)S(1)}, bf16[512,128]{1,0:T(8,128)(2,1)S(1)}, u32[]{:S(2)}, u32[]{:S(2)}) collective-permute-start(bf16[512,128]{1,0:T(8,128)(2,1)S(1)} %convert_element_type.9), channel_id=1, source_target_pairs={{0,2},{2,0},{4,6},{6,4},{8,10},{10,8},{12,14},{14,12},{16,18},{18,... | collective-permute-start | bytes 393224 | tf_op jit(solution)/shard_map/ppermute | solution.py:466
  85.2 4.7 %collective-permute-done.13.other = bf16[512,128]{1,0:T(8,128)(2,1)S(1)} collective-permute-done((bf16[512,128]{1,0:T(8,128)(2,1)S(1)}, bf16[512,128]{1,0:T(8,128)(2,1)S(1)}, u32[]{:S(2)}, u32[]{:S(2)}) %collective-permute-start.13) | collective-permute-done | bytes 131104 | tf_op jit(solution)/shard_map/ppermute | solution.py:466
  89.9 0.3 level_step.4.own.refs_5_
  90.3 5.2 %collective-permute-start.14 = (bf16[512,128]{1,0:T(8,128)(2,1)S(1)}, bf16[512,128]{1,0:T(8,128)(2,1)S(1)}, u32[]{:S(2)}, u32[]{:S(2)}) collective-permute-start(bf16[512,128]{1,0:T(8,128)(2,1)S(1)} %convert_element_type.10), channel_id=1, source_target_pairs={{0,4},{4,0},{8,12},{12,8},{16,20},{20,16},{24,28},{28,24},{32,36},... | collective-permute-start | bytes 393224 | tf_op jit(solution)/shard_map/ppermute | solution.py:466
  95.4 2.9 %collective-permute-done.14.other = bf16[512,128]{1,0:T(8,128)(2,1)S(1)} collective-permute-done((bf16[512,128]{1,0:T(8,128)(2,1)S(1)}, bf16[512,128]{1,0:T(8,128)(2,1)S(1)}, u32[]{:S(2)}, u32[]{:S(2)}) %collective-permute-start.14) | collective-permute-done | bytes 131104 | tf_op jit(solution)/shard_map/ppermute | solution.py:466
  98.4 0.3 level_step.5.refs_6_.v3
  98.7 8.1 %collective-permute-start.15 = (bf16[512,128]{1,0:T(8,128)(2,1)S(1)}, bf16[512,128]{1,0:T(8,128)(2,1)S(1)}, u32[]{:S(2)}, u32[]{:S(2)}) collective-permute-start(bf16[512,128]{1,0:T(8,128)(2,1)S(1)} %convert_element_type.11), channel_id=1, source_target_pairs={{0,8},{8,0},{16,24},{24,16},{32,40},{40,32},{48,56},{56,48},{64,72... | collective-permute-start | bytes 393224 | tf_op jit(solution)/shard_map/ppermute | solution.py:466
  106.8 6.0 %own_near.1.base = f32[512,2048]{1,0:T(8,128)S(1)} custom-call(s32[4,4]{1,0:T(4,128)S(1)} %copy-done.4, bf16[64,2048]{1,0:T(8,128)(2,1)S(1)} %copy-done.2, bf16[512,2048]{1,0:T(8,128)(2,1)S(1)} %copy-done, bf16[512,2048]{1,0:T(8,128)(2,1)S(1)} %copy-done.3), custom_call_target="tpu_custom_call" | custom-call | tf_op jit(solution)/shard_map/own_near/pallas_call | solution.py:325
  112.8 0.6 tables.1
  113.4 0.0 collective-permute-done.1.after
  113.4 2.9 %near_tiles.1.tiles = bf16[16,512,512]{2,1,0:T(8,128)(2,1)S(1)} custom-call(s32[4,4]{1,0:T(4,128)S(1)} %copy-done.4, bf16[64,2048]{1,0:T(8,128)(2,1)S(1)} %copy-done.2, bf16[256,2048]{1,0:T(8,128)(2,1)S(1)} %collective-permute-done.before, bf16[256,2048]{1,0:T(8,128)(2,1)S(1)} %collective-permute-done.1.after), custom_call_target="tpu_custom_call" | custom-call | tf_op jit(solution)/shard_map/near_tiles/pallas_call | solution.py:385
  116.3 3.4 %near_part.2 = (f32[192,2048]{1,0:T(8,128)S(1)}, f32[192,256]{1,0:T(8,128)S(1)}) custom-call(s32[4,4]{1,0:T(4,128)S(1)} %copy-done.4, f32[512,2048]{1,0:T(8,128)S(1)} %own_near.1.base, bf16[256,2048]{1,0:T(8,128)(2,1)S(1)} %collective-permute-done.before, bf16[256,2048]{1,0:T(8,128)(2,1)S(1)} %collective-permute-done.1.after, ...), custom_call_target="tpu_custom_call" | custom-call | tf_op jit(solution)/shard_map/near_part/pallas_call | solution.py:425
  119.7 4.1 %near_part.3 = (f32[320,2048]{1,0:T(8,128)S(1)}, f32[320,256]{1,0:T(8,128)S(1)}) custom-call(s32[4,4]{1,0:T(4,128)S(1)} %copy-done.4, f32[512,2048]{1,0:T(8,128)S(1)} %own_near.1.base, bf16[320,2048]{1,0:T(8,128)(2,1)S(1)} %collective-permute-done.6.before, bf16[320,2048]{1,0:T(8,128)(2,1)S(1)} %collective-permute-done.7.after, ...), custom_call_target="tpu_custom_call" | custom-call | tf_op jit(solution)/shard_map/near_part/pallas_call | solution.py:425
  123.9 1.9 %settle.1 = (f32[512,2048]{1,0:T(8,128)S(1)}, f32[512,256]{1,0:T(8,128)S(1)}) custom-call(s32[4,4]{1,0:T(4,128)S(1)} %copy-done.4, f32[192,2048]{1,0:T(8,128)S(1)} %get-tuple-element.28.refs_0_, f32[192,256]{1,0:T(8,128)S(1)} %get-tuple-element.29.refs_1_, f32[320,2048]{1,0:T(8,128)S(1)} %get-tuple-element.30.refs_2_, ...), custom_call_target="tpu_custom_call" | custom-call | tf_op jit(solution)/shard_map/settle/pallas_call | solution.py:490
  125.9 3.8 %finish.1 = f32[512,2048]{1,0:T(8,128)} custom-call(s32[4,4]{1,0:T(4,128)S(1)} %copy-done.4, f32[512,2048]{1,0:T(8,128)S(1)} %get-tuple-element.38.ready, f32[512,256]{1,0:T(8,128)S(1)} %get-tuple-element.39.corr, f32[512,128]{1,0:T(8,128)S(1)} %level_step.5.refs_6_.v3, bf16[512,128]{1,0:T(8,128)(2,1)S(1)} %collective-permute-done.15.w4, ...), custom_call_target="tpu_custom_call" | custom-call | tf_op jit(solution)/shard_map/finish/pallas_call | solution.py:526
  (17 shorter events, 0.1 us)
Async XLA Ops:
  0.0 0.9 copy-start.1
  1.0 0.7 copy-start.4
  1.6 0.7 copy-start.5
  3.5 14.8 %collective-permute-start.8 = (bf16[80,256]{1,0:T(8,128)(2,1)S(1)}, bf16[80,256]{1,0:T(8,128)(2,1)S(1)}, u32[]{:S(2)}, u32[]{:S(2)}) collective-permute-start(bf16[80,256]{1,0:T(8,128)(2,1)S(1)} %get-tuple-element.24.note), channel_id=1, source_target_pairs={{0,16},{16,32},{32,48},{48,64},{64,80},{80,96},{96,112},{112,128},... | collective-permute-start | bytes 122888 | tf_op jit(solution)/shard_map/ppermute | solution.py:540
  6.5 13.6 %collective-permute-start.9 = (bf16[80,256]{1,0:T(8,128)(2,1)S(1)}, bf16[80,256]{1,0:T(8,128)(2,1)S(1)}, u32[]{:S(2)}, u32[]{:S(2)}) collective-permute-start(bf16[80,256]{1,0:T(8,128)(2,1)S(1)} %get-tuple-element.24.note), channel_id=1, source_target_pairs={{16,0},{32,16},{48,32},{64,48},{80,64},{96,80},{112,96},{128,112},... | collective-permute-start | bytes 122888 | tf_op jit(solution)/shard_map/ppermute | solution.py:540
  9.3 14.2 %copy-start = (bf16[512,2048]{1,0:T(8,128)(2,1)S(1)}, bf16[512,2048]{1,0:T(8,128)(2,1)}, u32[]{:S(2)}) copy-start(bf16[512,2048]{1,0:T(8,128)(2,1)} %w.5) | copy-start | bytes 6291460
  9.3 18.8 %collective-permute-start.2 = (bf16[64,128]{1,0:T(8,128)(2,1)S(1)}, bf16[64,128]{1,0:T(8,128)(2,1)S(1)}, u32[]{:S(2)}, u32[]{:S(2)}) collective-permute-start(bf16[64,128]{1,0:T(8,128)(2,1)S(1)} %get-tuple-element.25.kept), channel_id=1, source_target_pairs={{0,1},{1,0},{2,3},{3,2},{4,5},{5,4},{6,7},{7,6},{8,9},{9,8},{10,11... | collective-permute-start | bytes 49160 | tf_op jit(solution)/shard_map/ppermute | solution.py:466
  9.4 23.3 %collective-permute-start.3 = (bf16[64,128]{1,0:T(8,128)(2,1)S(1)}, bf16[64,128]{1,0:T(8,128)(2,1)S(1)}, u32[]{:S(2)}, u32[]{:S(2)}) collective-permute-start(bf16[64,128]{1,0:T(8,128)(2,1)S(1)} %get-tuple-element.25.kept), channel_id=1, source_target_pairs={{0,2},{1,3},{2,0},{3,1},{4,6},{5,7},{6,4},{7,5},{8,10},{9,11},{10,... | collective-permute-start | bytes 49160 | tf_op jit(solution)/shard_map/ppermute | solution.py:466
  12.9 25.9 %slice-start = ((bf16[512,2048]{1,0:T(8,128)(2,1)}), bf16[192,2048]{1,0:T(8,128)(2,1)S(1)}, s32[]{:S(2)}) async-start(bf16[512,2048]{1,0:T(8,128)(2,1)} %w.5), calls=%async_computation | async-start | bytes 1572864 | tf_op jit(solution)/shard_map/slice | solution.py:556
  12.9 106.8 %collective-permute-start.6 = (bf16[320,2048]{1,0:T(8,128)(2,1)S(1)}, bf16[320,2048]{1,0:T(8,128)(2,1)S(1)}, u32[]{:S(2)}, u32[]{:S(2)}) collective-permute-start(bf16[320,2048]{1,0:T(8,128)(2,1)S(1)} %slice.7), channel_id=1, source_target_pairs={{0,16},{16,32},{32,48},{48,64},{64,80},{80,96},{96,112},{112,128},... | collective-permute-start | bytes 3932168 | tf_op jit(solution)/shard_map/ppermute | solution.py:540
  18.2 101.5 %collective-permute-start.7 = (bf16[320,2048]{1,0:T(8,128)(2,1)S(1)}, bf16[320,2048]{1,0:T(8,128)(2,1)S(1)}, u32[]{:S(2)}, u32[]{:S(2)}) collective-permute-start(bf16[320,2048]{1,0:T(8,128)(2,1)S(1)} %slice.7), channel_id=1, source_target_pairs={{16,0},{32,16},{48,32},{64,48},{80,64},{96,80},{112,96},{128,112},... | collective-permute-start | bytes 3932168 | tf_op jit(solution)/shard_map/ppermute | solution.py:540
  20.1 34.9 %copy-start.3 = (bf16[512,2048]{1,0:T(8,128)(2,1)S(1)}, bf16[512,2048]{1,0:T(8,128)(2,1)}, u32[]{:S(2)}) copy-start(bf16[512,2048]{1,0:T(8,128)(2,1)} %targets.3) | copy-start | bytes 6291460
  20.2 18.7 %collective-permute-start.4 = (bf16[64,128]{1,0:T(8,128)(2,1)S(1)}, bf16[64,128]{1,0:T(8,128)(2,1)S(1)}, u32[]{:S(2)}, u32[]{:S(2)}) collective-permute-start(bf16[64,128]{1,0:T(8,128)(2,1)S(1)} %get-tuple-element.25.kept), channel_id=1, source_target_pairs={{0,4},{1,5},{2,6},{3,7},{4,0},{5,1},{6,2},{7,3},{8,12},{9,13},{10,... | collective-permute-start | bytes 49160 | tf_op jit(solution)/shard_map/ppermute | solution.py:466
  28.2 12.7 %collective-permute-start.5 = (bf16[64,128]{1,0:T(8,128)(2,1)S(1)}, bf16[64,128]{1,0:T(8,128)(2,1)S(1)}, u32[]{:S(2)}, u32[]{:S(2)}) collective-permute-start(bf16[64,128]{1,0:T(8,128)(2,1)S(1)} %get-tuple-element.25.kept), channel_id=1, source_target_pairs={{0,8},{1,9},{2,10},{3,11},{4,12},{5,13},{6,14},{7,15},{8,0},{9,1},... | collective-permute-start | bytes 49160 | tf_op jit(solution)/shard_map/ppermute | solution.py:466
  32.7 20.2 %collective-permute-start.10 = (f32[512,128]{1,0:T(8,128)S(1)}, f32[512,128]{1,0:T(8,128)S(1)}, u32[]{:S(2)}, u32[]{:S(2)}) collective-permute-start(f32[512,128]{1,0:T(8,128)S(1)} %get-tuple-element.33), channel_id=1, source_target_pairs={{0,16},{16,32},{32,48},{48,64},{64,80},{80,96},{96,112},{112,128},... | collective-permute-start | bytes 786440 | tf_op jit(solution)/shard_map/ppermute | solution.py:540
  38.9 74.5 %collective-permute-start = (bf16[256,2048]{1,0:T(8,128)(2,1)S(1)}, bf16[256,2048]{1,0:T(8,128)(2,1)S(1)}, u32[]{:S(2)}, u32[]{:S(2)}) collective-permute-start(bf16[256,2048]{1,0:T(8,128)(2,1)S(1)} %pad_maximum_fusion), channel_id=1, source_target_pairs={{0,16},{16,32},{32,48},{48,64},{64,80},{80,96},{96,112},{112,128},... | collective-permute-start | bytes 3145736 | tf_op jit(solution)/shard_map/ppermute | solution.py:540
  40.8 72.6 %collective-permute-start.1 = (bf16[256,2048]{1,0:T(8,128)(2,1)S(1)}, bf16[256,2048]{1,0:T(8,128)(2,1)S(1)}, u32[]{:S(2)}, u32[]{:S(2)}) collective-permute-start(bf16[256,2048]{1,0:T(8,128)(2,1)S(1)} %pad_maximum_fusion), channel_id=1, source_target_pairs={{16,0},{32,16},{48,32},{64,48},{80,64},{96,80},{112,96},{128,112},... | collective-permute-start | bytes 3145736 | tf_op jit(solution)/shard_map/ppermute | solution.py:540
  53.0 27.9 %collective-permute-start.11 = (f32[512,128]{1,0:T(8,128)S(1)}, f32[512,128]{1,0:T(8,128)S(1)}, u32[]{:S(2)}, u32[]{:S(2)}) collective-permute-start(f32[512,128]{1,0:T(8,128)S(1)} %get-tuple-element.34), channel_id=1, source_target_pairs={{16,0},{32,16},{48,32},{64,48},{80,64},{96,80},{112,96},{128,112},... | collective-permute-start | bytes 786440 | tf_op jit(solution)/shard_map/ppermute | solution.py:540
  80.9 1.6 %collective-permute-start.12 = (f32[512,128]{1,0:T(8,128)S(1)}, f32[512,128]{1,0:T(8,128)S(1)}, u32[]{:S(2)}, u32[]{:S(2)}) collective-permute-start(f32[512,128]{1,0:T(8,128)S(1)} %join.1.own), channel_id=1, source_target_pairs={{0,1},{1,0},{2,3},{3,2},{4,5},{5,4},{6,7},{7,6},{8,9},{9,8},{10,11... | collective-permute-start | bytes 786440 | tf_op jit(solution)/shard_map/ppermute | solution.py:466
  82.9 23.9 %copy-start.2 = (bf16[64,2048]{1,0:T(8,128)(2,1)S(1)}, bf16[64,2048]{1,0:T(8,128)(2,1)}, u32[]{:S(2)}) copy-start(bf16[64,2048]{1,0:T(8,128)(2,1)} %pts.9) | copy-start | bytes 786436
  82.9 7.0 %collective-permute-start.13 = (bf16[512,128]{1,0:T(8,128)(2,1)S(1)}, bf16[512,128]{1,0:T(8,128)(2,1)S(1)}, u32[]{:S(2)}, u32[]{:S(2)}) collective-permute-start(bf16[512,128]{1,0:T(8,128)(2,1)S(1)} %convert_element_type.9), channel_id=1, source_target_pairs={{0,2},{2,0},{4,6},{6,4},{8,10},{10,8},{12,14},{14,12},{16,18},{18,... | collective-permute-start | bytes 393224 | tf_op jit(solution)/shard_map/ppermute | solution.py:466
  90.3 8.1 %collective-permute-start.14 = (bf16[512,128]{1,0:T(8,128)(2,1)S(1)}, bf16[512,128]{1,0:T(8,128)(2,1)S(1)}, u32[]{:S(2)}, u32[]{:S(2)}) collective-permute-start(bf16[512,128]{1,0:T(8,128)(2,1)S(1)} %convert_element_type.10), channel_id=1, source_target_pairs={{0,4},{4,0},{8,12},{12,8},{16,20},{20,16},{24,28},{28,24},{32,36},... | collective-permute-start | bytes 393224 | tf_op jit(solution)/shard_map/ppermute | solution.py:466
  98.7 27.1 %collective-permute-start.15 = (bf16[512,128]{1,0:T(8,128)(2,1)S(1)}, bf16[512,128]{1,0:T(8,128)(2,1)S(1)}, u32[]{:S(2)}, u32[]{:S(2)}) collective-permute-start(bf16[512,128]{1,0:T(8,128)(2,1)S(1)} %convert_element_type.11), channel_id=1, source_target_pairs={{0,8},{8,0},{16,24},{24,16},{32,40},{40,32},{48,56},{56,48},{64,72... | collective-permute-start | bytes 393224 | tf_op jit(solution)/shard_map/ppermute | solution.py:466

commit v3 on v2

--- a/solution.py
+++ b/solution.py
@@ -169,12 +169,15 @@
     return guesses
 
 
-def tree_part(total, w, left, right, ref, begin, j):
+def tree_part(total, w, left, right, ref, begin, j, ridge=None):
     features = ref.shape[0] - 16
     cols = slice(j * CLUSTER_PTS, (j + 1) * CLUSTER_PTS)
     flags = ref[features + begin + j : features + begin + j + 1, :].astype(f32)
     tile = kernel_of(left[cols, :], right, features) * flags
-    term = mm(w[:, cols], tile.astype(bf16))
+    tile = tile.astype(bf16)
+    if ridge is not None:
+        tile = tile + RIDGE * ridge[cols, :]
+    term = mm(w[:, cols], tile)
     if j == 0:
         total[...] = term
     else:
@@ -197,12 +200,12 @@
         pair_left, pair_right = lifted(jnp.concatenate([own, other[...]], axis=1))
         grams.append(kernel_of(pair_left, pair_right, features))
     jobs = [
-        functools.partial(tree_part, total, w, left, node_right, note, 2 * clusters, j)
+        functools.partial(tree_part, total, w, left, node_right, note, 2 * clusters, j, pick)
         for j in range(clusters)
     ]
 
     def rest():
-        total[...] = mm(targets[...], pick[...]) - RIDGE * mm(w[...], pick[...]) - total[...]
+        total[...] = mm(targets[...], pick[...]) - total[...]
 
     found = invert(grams, jobs + [rest], 1)
     ah, al = split(found[0])
@@ -484,20 +487,26 @@
         at += rows
 
 
-def settle(cuts, near_lists, parts, rest):
-    total = sum(cuts)
-    n = parts[0].shape[1]
-    return pl.pallas_call(
-        functools.partial(settle_kernel, cuts),
-        out_shape=(
-            jax.ShapeDtypeStruct((total, n), f32),
-            jax.ShapeDtypeStruct((total, parts[1].shape[1]), f32),
-        ),
-        in_specs=[SMEM] + [VMEM] * (len(parts) + len(rest)),
+def last_kernel(first, *refs):
+    lists, base, before, after, tiles, pick, a_high, a_low = refs[:8]
+    res_1, sol_1, v1, v2, v3, place, ready, corr, res, sol = refs[8:]
+    near_kernel(first, 0, lists, base, before, after, tiles, pick, a_high, a_low, res, sol)
+    cuts = (first, res.shape[0])
+    settle_kernel(cuts, lists, res_1, sol_1, res, sol, v1, v2, v3, place, ready, corr)
+
+
+def last_part(first, base, before, after, tiles, pick, a_high, a_low, near_lists, *rest):
+    total, n = base.shape
+    s = pick.shape[1]
+    return pl.pallas_call(
+        functools.partial(last_kernel, first),
+        out_shape=(jax.ShapeDtypeStruct((total, n), f32), jax.ShapeDtypeStruct((total, s), f32)),
+        in_specs=[SMEM] + [VMEM] * (7 + len(rest)),
         out_specs=(VMEM, VMEM),
-        compiler_params=params(),
-        name="settle",
-    )(near_lists, *parts, *rest)
+        scratch_shapes=[pltpu.VMEM((total - first, n), f32), pltpu.VMEM((total - first, s), f32)],
+        compiler_params=params(),
+        name="last_part",
+    )(near_lists, base, before, after, tiles, pick, a_high, a_low, *rest)
 
 
 def out_kernel(blocks, lists, ready, corr, v3, w4, b_high, b_low, tile, place, out, buf, sems):
@@ -546,8 +555,6 @@
 
 def on_device(points, weights, targets, near_lists, tile_counts, skeleton):
     features = points.shape[0]
-    rows = weights.shape[0]
-    late = rows - EARLY_ROWS
     size = lax.axis_size("leaf")
     steps = [[(i, i ^ (1 << k)) for i in range(0, size, 1 << k)] for k in range(4)]
 
@@ -571,16 +578,14 @@
     tiles = near_tiles(points, before_1, after_1, near_lists)
     shared = (tiles, pick, a_high, a_low, near_lists)
     res_1, sol_1 = near_part(0, EARLY_ROWS, features, base, before_1, after_1, *shared)
-    res_2, sol_2 = near_part(EARLY_ROWS, late, 0, base, before_2, after_2, *shared)
-
     tile, place = tables(points, note, pick)
 
     v1 = level_step(0, v0, among_leaves(v0, steps[0]), b_high, b_low)
     v2 = level_step(1, v1, among_leaves(v1.astype(bf16), steps[1]), b_high, b_low)
     v3 = level_step(2, v2, among_leaves(v2.astype(bf16), steps[2]), b_high, b_low)
     w4 = among_leaves(v3.astype(bf16), steps[3])
-    ready, corr = settle(
-        (EARLY_ROWS, late), near_lists, (res_1, sol_1, res_2, sol_2), (v1, v2, v3, place)
+    ready, corr = last_part(
+        EARLY_ROWS, base, before_2, after_2, *shared, res_1, sol_1, v1, v2, v3, place
     )
     return finish((192, 192, 128), near_lists, ready, corr, v3, w4, b_high, b_low, tile, place)
 

time: 130 us -> 131 us (level)
    pallas_call x1, Pallas kernels: 1.95 us -> 6.38 us  [last_part(): pl.pallas_call(functools.partial(last_kernel, first), out_shape=(jax.Shap...]
    pallas_call x2 -> x1, Pallas kernels: 7.53 us -> 3.4 us  [near_part(): pl.pallas_call(functools.partial(near_kernel, first, skip), out_shape=(ja...]
where the time goes in v3:
time: 131 us; the launch traced here: 130 us
  starting transfers between devices  52.7 us (40%)
  waiting for transfers between devices  37 us (28%)
  Pallas kernels  36 us (27%)
  local copies, waits for them, and re-layouts  3.78 us (3%)
    ppermute x8, waiting for transfers between devices, shifted(): return lax.ppermute(value, 'clus', pairs)  27.9 us
    ppermute x8, starting transfers between devices, shifted(): return lax.ppermute(value, 'clus', pairs)  27 us
    ppermute x8, starting transfers between devices, among_leaves(): return lax.ppermute(value, 'leaf', pairs)  25.7 us
    ppermute x8, waiting for transfers between devices, among_leaves(): return lax.ppermute(value, 'leaf', pairs)  9.14 us
    pallas_call x1, Pallas kernels, last_part(): pl.pallas_call(functools.partial(last_kernel, first), out_shape=(jax.Shap...  6.38 us
    pallas_call x1, Pallas kernels, inverses(): pl.pallas_call(inverse_kernel, out_shape=(jax.ShapeDtypeStruct((rows, hal...  6.11 us
    pallas_call x1, Pallas kernels, own_near(): pl.pallas_call(own_kernel, out_shape=jax.ShapeDtypeStruct(weights.shape,...  5.98 us
    pallas_call x1, Pallas kernels, push(): pl.pallas_call(push_kernel, out_shape=(jax.ShapeDtypeStruct((rows, s // 2...  4.6 us
  transfers between devices with their start and end apart: 16, of which 5 were waited for; matrix products, arithmetic and copies ran while one was open for 1% of the time, Pallas kernels for 24%

profile of v3, /device:TPU:24, one launch (start us, length us, event | category | flops | bytes accessed | tf_op | source)
XLA Modules:
  0.0 130.2 jit_solution(10155846665444603594)
XLA Ops:
  0.0 0.9 copy-done.1
  1.0 0.7 copy-done.4
  1.6 0.7 copy-done.5
  2.3 1.1 prep.1
  3.5 3.1 %collective-permute-start.8 = (bf16[80,256]{1,0:T(8,128)(2,1)S(1)}, bf16[80,256]{1,0:T(8,128)(2,1)S(1)}, u32[]{:S(2)}, u32[]{:S(2)}) collective-permute-start(bf16[80,256]{1,0:T(8,128)(2,1)S(1)} %get-tuple-element.22.note), channel_id=1, source_target_pairs={{0,16},{16,32},{32,48},{48,64},{64,80},{80,96},{96,112},{112,128},... | collective-permute-start | bytes 122888 | tf_op jit(solution)/shard_map/ppermute | solution.py:549
  6.5 2.8 %collective-permute-start.9 = (bf16[80,256]{1,0:T(8,128)(2,1)S(1)}, bf16[80,256]{1,0:T(8,128)(2,1)S(1)}, u32[]{:S(2)}, u32[]{:S(2)}) collective-permute-start(bf16[80,256]{1,0:T(8,128)(2,1)S(1)} %get-tuple-element.22.note), channel_id=1, source_target_pairs={{16,0},{32,16},{48,32},{64,48},{80,64},{96,80},{112,96},{128,112},... | collective-permute-start | bytes 122888 | tf_op jit(solution)/shard_map/ppermute | solution.py:549
  9.3 0.0 copy-start
  9.3 0.1 collective-permute-start.4
  9.4 2.0 %collective-permute-start.5 = (bf16[64,128]{1,0:T(8,128)(2,1)S(1)}, bf16[64,128]{1,0:T(8,128)(2,1)S(1)}, u32[]{:S(2)}, u32[]{:S(2)}) collective-permute-start(bf16[64,128]{1,0:T(8,128)(2,1)S(1)} %get-tuple-element.23.kept), channel_id=1, source_target_pairs={{0,2},{1,3},{2,0},{3,1},{4,6},{5,7},{6,4},{7,5},{8,10},{9,11},{10,... | collective-permute-start | bytes 49160 | tf_op jit(solution)/shard_map/ppermute | solution.py:469
  11.4 1.4 %slice.6 = bf16[320,2048]{1,0:T(8,128)(2,1)S(1)} slice(bf16[512,2048]{1,0:T(8,128)(2,1)} %w.5), slice={[192:512], [0:2048]} | slice | bytes 2621440 | tf_op jit(solution)/shard_map/slice | solution.py:568
  12.9 0.0 slice-start
  12.9 5.3 %collective-permute-start = (bf16[320,2048]{1,0:T(8,128)(2,1)S(1)}, bf16[320,2048]{1,0:T(8,128)(2,1)S(1)}, u32[]{:S(2)}, u32[]{:S(2)}) collective-permute-start(bf16[320,2048]{1,0:T(8,128)(2,1)S(1)} %slice.6), channel_id=1, source_target_pairs={{0,16},{16,32},{32,48},{48,64},{64,80},{80,96},{96,112},{112,128},... | collective-permute-start | bytes 3932168 | tf_op jit(solution)/shard_map/ppermute | solution.py:549
  18.2 0.0 collective-permute-done.8.note_b
  18.2 1.9 %collective-permute-start.1 = (bf16[320,2048]{1,0:T(8,128)(2,1)S(1)}, bf16[320,2048]{1,0:T(8,128)(2,1)S(1)}, u32[]{:S(2)}, u32[]{:S(2)}) collective-permute-start(bf16[320,2048]{1,0:T(8,128)(2,1)S(1)} %slice.6), channel_id=1, source_target_pairs={{16,0},{32,16},{48,32},{64,48},{80,64},{96,80},{112,96},{128,112},... | collective-permute-start | bytes 3932168 | tf_op jit(solution)/shard_map/ppermute | solution.py:549
  20.1 0.0 copy-start.3
  20.2 0.0 collective-permute-done.9.note_a
  20.2 3.4 %collective-permute-start.6 = (bf16[64,128]{1,0:T(8,128)(2,1)S(1)}, bf16[64,128]{1,0:T(8,128)(2,1)S(1)}, u32[]{:S(2)}, u32[]{:S(2)}) collective-permute-start(bf16[64,128]{1,0:T(8,128)(2,1)S(1)} %get-tuple-element.23.kept), channel_id=1, source_target_pairs={{0,4},{1,5},{2,6},{3,7},{4,0},{5,1},{6,2},{7,3},{8,12},{9,13},{10,... | collective-permute-start | bytes 49160 | tf_op jit(solution)/shard_map/ppermute | solution.py:469
  23.5 4.6 %push.1 = (f32[512,128]{1,0:T(8,128)S(1)}, f32[512,128]{1,0:T(8,128)S(1)}) custom-call(bf16[64,2048]{1,0:T(8,128)(2,1)S(1)} %copy-done.1, bf16[512,2048]{1,0:T(8,128)(2,1)S(1)} %copy-done, bf16[80,256]{1,0:T(8,128)(2,1)S(1)} %collective-permute-done.8.note_b, bf16[80,256]{1,0:T(8,128)(2,1)S(1)} %collective-permute-done.9.note_a), custom_call_target="tpu_custom_call" | custom-call | tf_op jit(solution)/shard_map/push/pallas_call | solution.py:258
  28.1 0.0 collective-permute-done.4.o1
  28.2 4.6 %collective-permute-start.7 = (bf16[64,128]{1,0:T(8,128)(2,1)S(1)}, bf16[64,128]{1,0:T(8,128)(2,1)S(1)}, u32[]{:S(2)}, u32[]{:S(2)}) collective-permute-start(bf16[64,128]{1,0:T(8,128)(2,1)S(1)} %get-tuple-element.23.kept), channel_id=1, source_target_pairs={{0,8},{1,9},{2,10},{3,11},{4,12},{5,13},{6,14},{7,15},{8,0},{9,1},... | collective-permute-start | bytes 49160 | tf_op jit(solution)/shard_map/ppermute | solution.py:469
  32.7 6.0 %collective-permute-start.10 = (f32[512,128]{1,0:T(8,128)S(1)}, f32[512,128]{1,0:T(8,128)S(1)}, u32[]{:S(2)}, u32[]{:S(2)}) collective-permute-start(f32[512,128]{1,0:T(8,128)S(1)} %get-tuple-element.29), channel_id=1, source_target_pairs={{0,16},{16,32},{32,48},{48,64},{64,80},{80,96},{96,112},{112,128},... | collective-permute-start | bytes 786440 | tf_op jit(solution)/shard_map/ppermute | solution.py:549
  38.8 0.1 pad_maximum_fusion
  38.9 0.0 collective-permute-done.6.o3
  38.9 1.9 %collective-permute-start.2 = (bf16[256,2048]{1,0:T(8,128)(2,1)S(1)}, bf16[256,2048]{1,0:T(8,128)(2,1)S(1)}, u32[]{:S(2)}, u32[]{:S(2)}) collective-permute-start(bf16[256,2048]{1,0:T(8,128)(2,1)S(1)} %pad_maximum_fusion), channel_id=1, source_target_pairs={{0,16},{16,32},{32,48},{48,64},{64,80},{80,96},{96,112},{112,128},... | collective-permute-start | bytes 3145736 | tf_op jit(solution)/shard_map/ppermute | solution.py:549
  40.8 3.9 %collective-permute-start.3 = (bf16[256,2048]{1,0:T(8,128)(2,1)S(1)}, bf16[256,2048]{1,0:T(8,128)(2,1)S(1)}, u32[]{:S(2)}, u32[]{:S(2)}) collective-permute-start(bf16[256,2048]{1,0:T(8,128)(2,1)S(1)} %pad_maximum_fusion), channel_id=1, source_target_pairs={{16,0},{32,16},{48,32},{64,48},{80,64},{96,80},{112,96},{128,112},... | collective-permute-start | bytes 3145736 | tf_op jit(solution)/shard_map/ppermute | solution.py:549
  44.8 8.2 %collective-permute-done.10.from_b = f32[512,128]{1,0:T(8,128)S(1)} collective-permute-done((f32[512,128]{1,0:T(8,128)S(1)}, f32[512,128]{1,0:T(8,128)S(1)}, u32[]{:S(2)}, u32[]{:S(2)}) %collective-permute-start.10) | collective-permute-done | bytes 262176 | tf_op jit(solution)/shard_map/ppermute | solution.py:549
  53.0 2.1 %collective-permute-start.11 = (f32[512,128]{1,0:T(8,128)S(1)}, f32[512,128]{1,0:T(8,128)S(1)}, u32[]{:S(2)}, u32[]{:S(2)}) collective-permute-start(f32[512,128]{1,0:T(8,128)S(1)} %get-tuple-element.30), channel_id=1, source_target_pairs={{16,0},{32,16},{48,32},{64,48},{80,64},{96,80},{112,96},{128,112},... | collective-permute-start | bytes 786440 | tf_op jit(solution)/shard_map/ppermute | solution.py:549
  55.1 6.1 %inverses.1 = (f32[512,128]{1,0:T(8,128)S(1)}, bf16[256,256]{1,0:T(8,128)(2,1)S(1)}, bf16[256,256]{1,0:T(8,128)(2,1)S(1)}, bf16[4,256,128]{2,1,0:T(8,128)(2,1)S(1)}, bf16[4,256,128]{2,1,0:T(8,128)(2,1)S(1)}) custom-call(bf16[64,2048]{1,0:T(8,128)(2,1)S(1)} %copy-done.1, bf16[512,2048]{1,0:T(8,128)(2,1)S(1)} %copy-done, bf16[512,2048]{1,0:T(8,128)(2,1)S(1)} %copy-done.3, ...), custom_call_target="tpu_custom_call" | custom-call | tf_op jit(solution)/shard_map/inverses/pallas_call | solution.py:225
  61.2 19.6 %collective-permute-done.11.from_a = f32[512,128]{1,0:T(8,128)S(1)} collective-permute-done((f32[512,128]{1,0:T(8,128)S(1)}, f32[512,128]{1,0:T(8,128)S(1)}, u32[]{:S(2)}, u32[]{:S(2)}) %collective-permute-start.11) | collective-permute-done | bytes 262176 | tf_op jit(solution)/shard_map/ppermute | solution.py:549
  80.9 0.1 collective-permute-start.12
  81.0 1.5 %collective-permute-done.12.other = f32[512,128]{1,0:T(8,128)S(1)} collective-permute-done((f32[512,128]{1,0:T(8,128)S(1)}, f32[512,128]{1,0:T(8,128)S(1)}, u32[]{:S(2)}, u32[]{:S(2)}) %collective-permute-start.12) | collective-permute-done | bytes 262176 | tf_op jit(solution)/shard_map/ppermute | solution.py:469
  82.5 0.4 level_step.3.own.refs_10_
  82.9 0.0 copy-start.2
  82.9 2.3 %collective-permute-start.13 = (bf16[512,128]{1,0:T(8,128)(2,1)S(1)}, bf16[512,128]{1,0:T(8,128)(2,1)S(1)}, u32[]{:S(2)}, u32[]{:S(2)}) collective-permute-start(bf16[512,128]{1,0:T(8,128)(2,1)S(1)} %convert_element_type.9), channel_id=1, source_target_pairs={{0,2},{2,0},{4,6},{6,4},{8,10},{10,8},{12,14},{14,12},{16,18},{18,... | collective-permute-start | bytes 393224 | tf_op jit(solution)/shard_map/ppermute | solution.py:469
  85.2 4.7 %collective-permute-done.13.other = bf16[512,128]{1,0:T(8,128)(2,1)S(1)} collective-permute-done((bf16[512,128]{1,0:T(8,128)(2,1)S(1)}, bf16[512,128]{1,0:T(8,128)(2,1)S(1)}, u32[]{:S(2)}, u32[]{:S(2)}) %collective-permute-start.13) | collective-permute-done | bytes 131104 | tf_op jit(solution)/shard_map/ppermute | solution.py:469
  89.9 0.3 level_step.4.own.refs_11_
  90.3 5.2 %collective-permute-start.14 = (bf16[512,128]{1,0:T(8,128)(2,1)S(1)}, bf16[512,128]{1,0:T(8,128)(2,1)S(1)}, u32[]{:S(2)}, u32[]{:S(2)}) collective-permute-start(bf16[512,128]{1,0:T(8,128)(2,1)S(1)} %convert_element_type.10), channel_id=1, source_target_pairs={{0,4},{4,0},{8,12},{12,8},{16,20},{20,16},{24,28},{28,24},{32,36},... | collective-permute-start | bytes 393224 | tf_op jit(solution)/shard_map/ppermute | solution.py:469
  95.5 2.9 %collective-permute-done.14.other = bf16[512,128]{1,0:T(8,128)(2,1)S(1)} collective-permute-done((bf16[512,128]{1,0:T(8,128)(2,1)S(1)}, bf16[512,128]{1,0:T(8,128)(2,1)S(1)}, u32[]{:S(2)}, u32[]{:S(2)}) %collective-permute-start.14) | collective-permute-done | bytes 131104 | tf_op jit(solution)/shard_map/ppermute | solution.py:469
  98.4 0.3 level_step.5.refs_12_.v3
  98.7 8.1 %collective-permute-start.15 = (bf16[512,128]{1,0:T(8,128)(2,1)S(1)}, bf16[512,128]{1,0:T(8,128)(2,1)S(1)}, u32[]{:S(2)}, u32[]{:S(2)}) collective-permute-start(bf16[512,128]{1,0:T(8,128)(2,1)S(1)} %convert_element_type.11), channel_id=1, source_target_pairs={{0,8},{8,0},{16,24},{24,16},{32,40},{40,32},{48,56},{56,48},{64,72... | collective-permute-start | bytes 393224 | tf_op jit(solution)/shard_map/ppermute | solution.py:469
  106.8 6.0 %own_near.1.base.refs_1_ = f32[512,2048]{1,0:T(8,128)S(1)} custom-call(s32[4,4]{1,0:T(4,128)S(1)} %copy-done.4, bf16[64,2048]{1,0:T(8,128)(2,1)S(1)} %copy-done.2, bf16[512,2048]{1,0:T(8,128)(2,1)S(1)} %copy-done, bf16[512,2048]{1,0:T(8,128)(2,1)S(1)} %copy-done.3), custom_call_target="tpu_custom_call" | custom-call | tf_op jit(solution)/shard_map/own_near/pallas_call | solution.py:328
  112.8 0.6 tables.1
  113.4 0.0 collective-permute-done.2.before
  113.4 2.9 %near_tiles.1.tiles.refs_4_ = bf16[16,512,512]{2,1,0:T(8,128)(2,1)S(1)} custom-call(s32[4,4]{1,0:T(4,128)S(1)} %copy-done.4, bf16[64,2048]{1,0:T(8,128)(2,1)S(1)} %copy-done.2, bf16[256,2048]{1,0:T(8,128)(2,1)S(1)} %collective-permute-done.2.before, bf16[256,2048]{1,0:T(8,128)(2,1)S(1)} %collective-permute-done.3.after), custom_call_target="tpu_custom_call" | custom-call | tf_op jit(solution)/shard_map/near_tiles/pallas_call | solution.py:388
  116.3 3.4 %near_part.1 = (f32[192,2048]{1,0:T(8,128)S(1)}, f32[192,256]{1,0:T(8,128)S(1)}) custom-call(s32[4,4]{1,0:T(4,128)S(1)} %copy-done.4, f32[512,2048]{1,0:T(8,128)S(1)} %own_near.1.base.refs_1_, bf16[256,2048]{1,0:T(8,128)(2,1)S(1)} %collective-permute-done.2.before, bf16[256,2048]{1,0:T(8,128)(2,1)S(1)} %collective-permute-done.3.after, ...), custom_call_target="tpu_custom_call" | custom-call | tf_op jit(solution)/shard_map/near_part/pallas_call | solution.py:428
  119.7 0.0 collective-permute-done.refs_2_
  119.8 6.4 %last_part.1 = (f32[512,2048]{1,0:T(8,128)S(1)}, f32[512,256]{1,0:T(8,128)S(1)}) custom-call(s32[4,4]{1,0:T(4,128)S(1)} %copy-done.4, f32[512,2048]{1,0:T(8,128)S(1)} %own_near.1.base.refs_1_, bf16[320,2048]{1,0:T(8,128)(2,1)S(1)} %collective-permute-done.refs_2_, bf16[320,2048]{1,0:T(8,128)(2,1)S(1)} %collective-permute-done.1.refs_3_, ...), custom_call_target="tpu_custom_call" | custom-call | tf_op jit(solution)/shard_map/last_part/pallas_call | solution.py:501
  126.2 3.8 %finish.1 = f32[512,2048]{1,0:T(8,128)} custom-call(s32[4,4]{1,0:T(4,128)S(1)} %copy-done.4, f32[512,2048]{1,0:T(8,128)S(1)} %get-tuple-element.34.ready, f32[512,256]{1,0:T(8,128)S(1)} %get-tuple-element.35.corr, f32[512,128]{1,0:T(8,128)S(1)} %level_step.5.refs_12_.v3, bf16[512,128]{1,0:T(8,128)(2,1)S(1)} %collective-permute-done.15.w4, ...), custom_call_target="tpu_custom_call" | custom-call | tf_op jit(solution)/shard_map/finish/pallas_call | solution.py:535
  (16 shorter events, 0.1 us)
Async XLA Ops:
  0.0 0.9 copy-start.1
  1.0 0.7 copy-start.4
  1.6 0.7 copy-start.5
  3.5 14.8 %collective-permute-start.8 = (bf16[80,256]{1,0:T(8,128)(2,1)S(1)}, bf16[80,256]{1,0:T(8,128)(2,1)S(1)}, u32[]{:S(2)}, u32[]{:S(2)}) collective-permute-start(bf16[80,256]{1,0:T(8,128)(2,1)S(1)} %get-tuple-element.22.note), channel_id=1, source_target_pairs={{0,16},{16,32},{32,48},{48,64},{64,80},{80,96},{96,112},{112,128},... | collective-permute-start | bytes 122888 | tf_op jit(solution)/shard_map/ppermute | solution.py:549
  6.5 13.6 %collective-permute-start.9 = (bf16[80,256]{1,0:T(8,128)(2,1)S(1)}, bf16[80,256]{1,0:T(8,128)(2,1)S(1)}, u32[]{:S(2)}, u32[]{:S(2)}) collective-permute-start(bf16[80,256]{1,0:T(8,128)(2,1)S(1)} %get-tuple-element.22.note), channel_id=1, source_target_pairs={{16,0},{32,16},{48,32},{64,48},{80,64},{96,80},{112,96},{128,112},... | collective-permute-start | bytes 122888 | tf_op jit(solution)/shard_map/ppermute | solution.py:549
  9.3 14.2 %copy-start = (bf16[512,2048]{1,0:T(8,128)(2,1)S(1)}, bf16[512,2048]{1,0:T(8,128)(2,1)}, u32[]{:S(2)}) copy-start(bf16[512,2048]{1,0:T(8,128)(2,1)} %w.5) | copy-start | bytes 6291460
  9.3 18.8 %collective-permute-start.4 = (bf16[64,128]{1,0:T(8,128)(2,1)S(1)}, bf16[64,128]{1,0:T(8,128)(2,1)S(1)}, u32[]{:S(2)}, u32[]{:S(2)}) collective-permute-start(bf16[64,128]{1,0:T(8,128)(2,1)S(1)} %get-tuple-element.23.kept), channel_id=1, source_target_pairs={{0,1},{1,0},{2,3},{3,2},{4,5},{5,4},{6,7},{7,6},{8,9},{9,8},{10,11... | collective-permute-start | bytes 49160 | tf_op jit(solution)/shard_map/ppermute | solution.py:469
  9.4 23.3 %collective-permute-start.5 = (bf16[64,128]{1,0:T(8,128)(2,1)S(1)}, bf16[64,128]{1,0:T(8,128)(2,1)S(1)}, u32[]{:S(2)}, u32[]{:S(2)}) collective-permute-start(bf16[64,128]{1,0:T(8,128)(2,1)S(1)} %get-tuple-element.23.kept), channel_id=1, source_target_pairs={{0,2},{1,3},{2,0},{3,1},{4,6},{5,7},{6,4},{7,5},{8,10},{9,11},{10,... | collective-permute-start | bytes 49160 | tf_op jit(solution)/shard_map/ppermute | solution.py:469
  12.9 25.9 %slice-start = ((bf16[512,2048]{1,0:T(8,128)(2,1)}), bf16[192,2048]{1,0:T(8,128)(2,1)S(1)}, s32[]{:S(2)}) async-start(bf16[512,2048]{1,0:T(8,128)(2,1)} %w.5), calls=%async_computation | async-start | bytes 1572864 | tf_op jit(solution)/shard_map/slice | solution.py:563
  12.9 106.9 %collective-permute-start = (bf16[320,2048]{1,0:T(8,128)(2,1)S(1)}, bf16[320,2048]{1,0:T(8,128)(2,1)S(1)}, u32[]{:S(2)}, u32[]{:S(2)}) collective-permute-start(bf16[320,2048]{1,0:T(8,128)(2,1)S(1)} %slice.6), channel_id=1, source_target_pairs={{0,16},{16,32},{32,48},{48,64},{64,80},{80,96},{96,112},{112,128},... | collective-permute-start | bytes 3932168 | tf_op jit(solution)/shard_map/ppermute | solution.py:549
  18.2 101.5 %collective-permute-start.1 = (bf16[320,2048]{1,0:T(8,128)(2,1)S(1)}, bf16[320,2048]{1,0:T(8,128)(2,1)S(1)}, u32[]{:S(2)}, u32[]{:S(2)}) collective-permute-start(bf16[320,2048]{1,0:T(8,128)(2,1)S(1)} %slice.6), channel_id=1, source_target_pairs={{16,0},{32,16},{48,32},{64,48},{80,64},{96,80},{112,96},{128,112},... | collective-permute-start | bytes 3932168 | tf_op jit(solution)/shard_map/ppermute | solution.py:549
  20.1 34.9 %copy-start.3 = (bf16[512,2048]{1,0:T(8,128)(2,1)S(1)}, bf16[512,2048]{1,0:T(8,128)(2,1)}, u32[]{:S(2)}) copy-start(bf16[512,2048]{1,0:T(8,128)(2,1)} %targets.3) | copy-start | bytes 6291460
  20.2 18.7 %collective-permute-start.6 = (bf16[64,128]{1,0:T(8,128)(2,1)S(1)}, bf16[64,128]{1,0:T(8,128)(2,1)S(1)}, u32[]{:S(2)}, u32[]{:S(2)}) collective-permute-start(bf16[64,128]{1,0:T(8,128)(2,1)S(1)} %get-tuple-element.23.kept), channel_id=1, source_target_pairs={{0,4},{1,5},{2,6},{3,7},{4,0},{5,1},{6,2},{7,3},{8,12},{9,13},{10,... | collective-permute-start | bytes 49160 | tf_op jit(solution)/shard_map/ppermute | solution.py:469
  28.2 12.7 %collective-permute-start.7 = (bf16[64,128]{1,0:T(8,128)(2,1)S(1)}, bf16[64,128]{1,0:T(8,128)(2,1)S(1)}, u32[]{:S(2)}, u32[]{:S(2)}) collective-permute-start(bf16[64,128]{1,0:T(8,128)(2,1)S(1)} %get-tuple-element.23.kept), channel_id=1, source_target_pairs={{0,8},{1,9},{2,10},{3,11},{4,12},{5,13},{6,14},{7,15},{8,0},{9,1},... | collective-permute-start | bytes 49160 | tf_op jit(solution)/shard_map/ppermute | solution.py:469
  32.7 20.2 %collective-permute-start.10 = (f32[512,128]{1,0:T(8,128)S(1)}, f32[512,128]{1,0:T(8,128)S(1)}, u32[]{:S(2)}, u32[]{:S(2)}) collective-permute-start(f32[512,128]{1,0:T(8,128)S(1)} %get-tuple-element.29), channel_id=1, source_target_pairs={{0,16},{16,32},{32,48},{48,64},{64,80},{80,96},{96,112},{112,128},... | collective-permute-start | bytes 786440 | tf_op jit(solution)/shard_map/ppermute | solution.py:549
  38.9 74.5 %collective-permute-start.2 = (bf16[256,2048]{1,0:T(8,128)(2,1)S(1)}, bf16[256,2048]{1,0:T(8,128)(2,1)S(1)}, u32[]{:S(2)}, u32[]{:S(2)}) collective-permute-start(bf16[256,2048]{1,0:T(8,128)(2,1)S(1)} %pad_maximum_fusion), channel_id=1, source_target_pairs={{0,16},{16,32},{32,48},{48,64},{64,80},{80,96},{96,112},{112,128},... | collective-permute-start | bytes 3145736 | tf_op jit(solution)/shard_map/ppermute | solution.py:549
  40.8 72.6 %collective-permute-start.3 = (bf16[256,2048]{1,0:T(8,128)(2,1)S(1)}, bf16[256,2048]{1,0:T(8,128)(2,1)S(1)}, u32[]{:S(2)}, u32[]{:S(2)}) collective-permute-start(bf16[256,2048]{1,0:T(8,128)(2,1)S(1)} %pad_maximum_fusion), channel_id=1, source_target_pairs={{16,0},{32,16},{48,32},{64,48},{80,64},{96,80},{112,96},{128,112},... | collective-permute-start | bytes 3145736 | tf_op jit(solution)/shard_map/ppermute | solution.py:549
  53.0 27.9 %collective-permute-start.11 = (f32[512,128]{1,0:T(8,128)S(1)}, f32[512,128]{1,0:T(8,128)S(1)}, u32[]{:S(2)}, u32[]{:S(2)}) collective-permute-start(f32[512,128]{1,0:T(8,128)S(1)} %get-tuple-element.30), channel_id=1, source_target_pairs={{16,0},{32,16},{48,32},{64,48},{80,64},{96,80},{112,96},{128,112},... | collective-permute-start | bytes 786440 | tf_op jit(solution)/shard_map/ppermute | solution.py:549
  80.9 1.6 %collective-permute-start.12 = (f32[512,128]{1,0:T(8,128)S(1)}, f32[512,128]{1,0:T(8,128)S(1)}, u32[]{:S(2)}, u32[]{:S(2)}) collective-permute-start(f32[512,128]{1,0:T(8,128)S(1)} %join.1.own), channel_id=1, source_target_pairs={{0,1},{1,0},{2,3},{3,2},{4,5},{5,4},{6,7},{7,6},{8,9},{9,8},{10,11... | collective-permute-start | bytes 786440 | tf_op jit(solution)/shard_map/ppermute | solution.py:469
  82.9 23.9 %copy-start.2 = (bf16[64,2048]{1,0:T(8,128)(2,1)S(1)}, bf16[64,2048]{1,0:T(8,128)(2,1)}, u32[]{:S(2)}) copy-start(bf16[64,2048]{1,0:T(8,128)(2,1)} %pts.9) | copy-start | bytes 786436
  82.9 7.0 %collective-permute-start.13 = (bf16[512,128]{1,0:T(8,128)(2,1)S(1)}, bf16[512,128]{1,0:T(8,128)(2,1)S(1)}, u32[]{:S(2)}, u32[]{:S(2)}) collective-permute-start(bf16[512,128]{1,0:T(8,128)(2,1)S(1)} %convert_element_type.9), channel_id=1, source_target_pairs={{0,2},{2,0},{4,6},{6,4},{8,10},{10,8},{12,14},{14,12},{16,18},{18,... | collective-permute-start | bytes 393224 | tf_op jit(solution)/shard_map/ppermute | solution.py:469
  90.3 8.1 %collective-permute-start.14 = (bf16[512,128]{1,0:T(8,128)(2,1)S(1)}, bf16[512,128]{1,0:T(8,128)(2,1)S(1)}, u32[]{:S(2)}, u32[]{:S(2)}) collective-permute-start(bf16[512,128]{1,0:T(8,128)(2,1)S(1)} %convert_element_type.10), channel_id=1, source_target_pairs={{0,4},{4,0},{8,12},{12,8},{16,20},{20,16},{24,28},{28,24},{32,36},... | collective-permute-start | bytes 393224 | tf_op jit(solution)/shard_map/ppermute | solution.py:469
  98.7 27.4 %collective-permute-start.15 = (bf16[512,128]{1,0:T(8,128)(2,1)S(1)}, bf16[512,128]{1,0:T(8,128)(2,1)S(1)}, u32[]{:S(2)}, u32[]{:S(2)}) collective-permute-start(bf16[512,128]{1,0:T(8,128)(2,1)S(1)} %convert_element_type.11), channel_id=1, source_target_pairs={{0,8},{8,0},{16,24},{24,16},{32,40},{40,32},{48,56},{56,48},{64,72... | collective-permute-start | bytes 393224 | tf_op jit(solution)/shard_map/ppermute | solution.py:469
